TPU v7x, 512 devices: a whole 4x4x16 slice. The times are simulated.
512 devices in a mesh: rows: 128 (over y, x, z_lo), rep: 4 (over z_hi, core).
Axes of the slice: x: 4, y: 4, z: 16 (z_hi: 2, z_lo: 8; z = z_hi * 8 + z_lo), core: 2. Of those that a mesh axis runs over, the one named last changes fastest.
Arguments:
- covariates: bfloat16 [1048576, 128], P(('rows', 'rep')), may hold values from -6 to 6
- treated: int32 [1048576], P(('rows', 'rep')), may hold values 0 or 1
- landmarks: bfloat16 [1024, 128], P('rows'), may hold values from -6 to 6
- land_treat: bfloat16 [1024], P('rows'), may hold values from 0 to 1
Outputs:
- gram: float32 [1024, 512], P('rows')
- moment: float32 [1024], P('rows')
All inputs are finite; a program needn't handle non-finite values. No bound on the sum of `treated` on one device may be relied on, other than what follows from the above.
Results may differ from a plain program's by a relative error of at most 0.0034.
Values may be sent and summed in bfloat16 or wider, within the bound.
No kernel may reach another device: no remote copies, remote signals or barrier semaphores. Data moves between devices by JAX's collectives and lax.ppermute only.
A program may use at most 64 MiB of HBM per device.

v0:
```python
import jax
import jax.numpy as jnp
from jax import lax
from jax.sharding import PartitionSpec as P

PANELS = 2


gamma_rate = 0.03125


def on_device(covariates, treated, landmarks, land_treat):
    width = covariates.shape[1]
    total_rows = covariates.shape[0] * lax.axis_size("rows") * lax.axis_size("rep")
    all_land, all_treat = (
        lax.all_gather(landmarks, "rows", axis=0, tiled=True),
        lax.all_gather(land_treat, "rows", axis=0, tiled=True),
    )
    rows_f = covariates.astype(jnp.float32)
    sq_rows = jnp.sum(rows_f * rows_f, axis=1)[:, None]
    land_f = all_land.astype(jnp.float32)
    sq_land = jnp.sum(land_f * land_f, axis=1)
    lt_value = all_treat.astype(jnp.float32)
    on_one = jnp.exp(-0.5 * jnp.square(1.0 - lt_value))
    on_zero = jnp.exp(-0.5 * jnp.square(lt_value))
    is_treated = treated[:, None] == 1
    panel_size = all_land.shape[0] // PANELS
    gram_terms = []
    kern_terms = []
    for panel in range(PANELS):
        first = panel * panel_size
        block = all_land[first : first + panel_size]
        cross = lax.dot_general(
            covariates, block, (((1,), (1,)), ((), ())), preferred_element_type=jnp.float32
        )
        kern = jnp.exp(
            gamma_rate
            * (2.0 * width - sq_rows - sq_land[None, first : first + panel_size] + 2.0 * cross)
        )
        factor = jnp.where(
            is_treated,
            on_one[None, first : first + panel_size],
            on_zero[None, first : first + panel_size],
        )
        features = (kern * factor).astype(jnp.bfloat16)
        gram_part = lax.dot_general(
            features, features, (((0,), (0,)), ((), ())), preferred_element_type=jnp.float32
        )
        gram_terms.append(gram_part / total_rows)
        kern_terms.append(jnp.sum(kern, axis=0) / total_rows)
    gram_term = jnp.concatenate(gram_terms, axis=0)
    moment_term = (on_one - on_zero) * jnp.concatenate(kern_terms, axis=0)
    shares = (
        lax.psum_scatter(gram_term, "rows", scatter_dimension=0, tiled=True),
        lax.psum_scatter(moment_term, "rows", scatter_dimension=0, tiled=True),
    )
    gram_out, moment_out = lax.psum((shares[0], shares[1]), "rep")
    return (gram_out, moment_out)


def solution(mesh):
    in_specs = (P(("rows", "rep"), None), P(("rows", "rep")), P("rows", None), P("rows"))
    out_specs = (P("rows", None), P("rows"))
    return jax.shard_map(
        on_device, mesh=mesh, in_specs=in_specs, out_specs=out_specs, check_vma=False
    )
```

profile of v0, /device:TPU:1, one launch (start us, length us, event | category | flops | bytes accessed | tf_op | source)
XLA Modules:
  0.0 2144.9 jit_solution(338041234744841244)
XLA Ops:
  7.2 0.0 copy-start
  7.2 0.0 reduce-scatter.2.cloned.1.call-start
  7.2 0.7 broadcast_compare_fusion
  8.0 1.3 fusion.20
  10.0 0.8 dynamic-update-slice
  10.8 477.4 %all-reduce = bf16[1024]{0:T(1024)(128)(2,1)S(1)} all-reduce(bf16[1024]{0:T(1024)(128)(2,1)S(1)} %dynamic-update-slice), channel_id=1, replica_groups=mesh['rows'=128,'rep'=4] {'rows'}, use_global_device_ids=true, to_apply=%add | all-reduce | flops 1024 | bytes 4096
  488.3 1.4 multiply_reduce_fusion
  489.7 457.1 %all_gather.6 = bf16[1024,128]{1,0:T(8,128)(2,1)S(1)} all-gather(bf16[8,128]{1,0:T(8,128)(2,1)} %param.6), channel_id=1, replica_groups=mesh['rows'=128,'rep'=4] {'rows'}, dimensions={0}, use_global_device_ids=true | all-gather | bytes 264192 | tf_op jit(solution)/shard_map/all_gather | solution.py:16
  946.7 0.2 multiply_reduce_fusion.1
  947.0 2.2 fusion.22
  949.2 0.0 copy-done
  949.2 1.1 fusion.21
  950.4 2.0 fusion.8
  952.3 2.0 fusion.9
  954.3 1.5 pad_maximum_fusion
  955.9 0.0 reduce-scatter.2.cloned.1.call-update
  956.5 463.3 %all-reduce.1 = f32[1024]{0:T(1024)S(1)} all-reduce(f32[1024]{0:T(1024)S(1)} %get-tuple-element.12), channel_id=3, replica_groups=mesh['rows'=128,'rep'=4] {'rows'}, use_global_device_ids=true, to_apply=%region_6.7.clone | all-reduce | flops 1024 | bytes 8192
  1419.8 0.1 dynamic-slice.2
  1419.9 584.4 %reduce-scatter.2.cloned.1.call-done = f32[8,512]{1,0:T(8,128)} async-done(((f32[1024,512]{1,0:T(8,128)}), f32[8,512]{1,0:T(8,128)}) %reduce-scatter.2.cloned.1.call-update) | async-done | bytes 16400 | tf_op jit(solution)/shard_map/reduce_scatter | solution.py:54
  2004.3 133.8 %all-reduce.2 = (f32[8,512]{1,0:T(8,128)}, f32[8]{0:T(128)}) all-reduce(f32[8,512]{1,0:T(8,128)} %reduce-scatter.2.cloned.1.call-done, f32[8]{0:T(128)S(1)} %dynamic-slice.2), channel_id=1, replica_groups=mesh['rows'=128,'rep'=4] {'rep'}, use_global_device_ids=true, to_apply=%region_3.4 | all-reduce | flops 4104 | bytes 32832 | tf_op jit(solution)/shard_map/psum | solution.py:57
  (7 shorter events, 0.0 us)
Async XLA Ops:
  7.2 942.0 %copy-start = (bf16[2048,128]{1,0:T(8,128)(2,1)S(1)}, bf16[2048,128]{1,0:T(8,128)(2,1)}, u32[]{:S(2)}) copy-start(bf16[2048,128]{1,0:T(8,128)(2,1)} %param.4) | copy-start | bytes 1572868
  7.2 1997.1 %reduce-scatter.2.cloned.1.call-start = ((), (), s32[]{:S(2)}) async-start(), calls=%async_computation.1 | async-start | bytes 2113536 | tf_op jit(solution)/shard_map/reduce_scatter | solution.py:54
Sparse Core Ops, SparseCore 0:
  956.0 1048.2 reduce-scatter.1
where the time goes:
time: 2150 us; the launch traced here: 2140 us
  blocking collectives  1530 us (71%)
  waiting for transfers between devices  584 us (27%)
    unnamed x2, blocking collectives  941 us
    reduce_scatter x1, waiting for transfers between devices, on_device(): lax.psum_scatter(gram_term, 'rows', scatter_dimension=0, tiled=True)  584 us
    all_gather x1, blocking collectives, on_device(): lax.all_gather(landmarks, 'rows', axis=0, tiled=True)  457 us
    psum x1, blocking collectives, on_device(): gram_out, moment_out = lax.psum((shares[0], shares[1]), 'rep')  134 us
  transfers between devices with their start and end apart: 1, of which 1 were waited for; matrix products, arithmetic and copies ran while one was open for 0% of the time, Pallas kernels for 0%

commit v1 on v0

v1 whole, which is shorter than its diff:
```python
import jax
import jax.numpy as jnp
from jax import lax
from jax.sharding import Mesh, PartitionSpec as P

PANELS = 2
Y, X, ZL, ZH, CORE = 4, 4, 8, 2, 2
PLANE = ("y", "x")
RING = ("zh", "zl")

gamma_rate = 0.03125


def spread(block, axes, count):
    copies = jnp.broadcast_to(block[None], (count,) + block.shape)
    return lax.all_to_all(copies, axes, 0, 0)


def on_device(covariates, treated, landmarks, land_treat):
    width = covariates.shape[1]
    total_rows = covariates.shape[0] * Y * X * ZL * ZH * CORE
    own = landmarks.shape[0]
    treat_row = jnp.zeros((8, width), landmarks.dtype).at[0, :own].set(land_treat)
    run = spread(jnp.concatenate([landmarks, treat_row], axis=0), "zl", ZL)
    run_treat = run[:, own, :own].reshape(1, ZL * own)
    run_treat = jnp.pad(run_treat, ((0, 7), (0, width - ZL * own)))
    run_block = jnp.concatenate([run[:, :own].reshape(ZL * own, width), run_treat], axis=0)
    plane = spread(run_block, PLANE, Y * X)
    all_land = plane[:, : ZL * own].reshape(-1, width)
    all_treat = plane[:, ZL * own, : ZL * own].reshape(-1)

    rows_f = covariates.astype(jnp.float32)
    sq_rows = jnp.sum(rows_f * rows_f, axis=1)[:, None]
    land_f = all_land.astype(jnp.float32)
    sq_land = jnp.sum(land_f * land_f, axis=1)
    lt_value = all_treat.astype(jnp.float32)
    on_one = jnp.exp(-0.5 * jnp.square(1.0 - lt_value))
    on_zero = jnp.exp(-0.5 * jnp.square(lt_value))
    is_treated = treated[:, None] == 1
    panel_size = all_land.shape[0] // PANELS
    half = panel_size // CORE
    core = lax.axis_index("core")
    sends, keeps, kern_terms = [], [], []
    for panel in range(PANELS):
        first = panel * panel_size
        block = all_land[first : first + panel_size]
        cross = lax.dot_general(
            covariates, block, (((1,), (1,)), ((), ())), preferred_element_type=jnp.float32
        )
        kern = jnp.exp(
            gamma_rate
            * (2.0 * width - sq_rows - sq_land[None, first : first + panel_size] + 2.0 * cross)
        )
        factor = jnp.where(
            is_treated,
            on_one[None, first : first + panel_size],
            on_zero[None, first : first + panel_size],
        )
        features = (kern * factor).astype(jnp.bfloat16)
        gram = lax.dot_general(
            features, features, (((0,), (0,)), ((), ())), preferred_element_type=jnp.float32
        )
        sends.append(lax.dynamic_slice(gram, (0, (1 - core) * half), (panel_size, half)))
        keeps.append(lax.dynamic_slice(gram, (0, core * half), (panel_size, half)))
        kern_terms.append(jnp.sum(kern, axis=0))
    send = jnp.concatenate(sends, axis=0).astype(jnp.bfloat16)
    keep = jnp.concatenate(keeps, axis=0)
    got = lax.ppermute(send, "core", [(0, 1), (1, 0)])
    pair = (keep + got.astype(jnp.float32)).astype(jnp.bfloat16).reshape(Y * X, ZL * own, half)
    kern_sum = jnp.concatenate(kern_terms, axis=0).astype(jnp.bfloat16).reshape(Y * X, 1, ZL * own)
    kern_sum = jnp.pad(kern_sum, ((0, 0), (0, 7), (0, half - ZL * own)))
    mine = lax.all_to_all(jnp.concatenate([pair, kern_sum], axis=1), PLANE, 0, 0)
    mine = jnp.sum(mine.astype(jnp.float32), axis=0)
    gram_z = mine[: ZL * own].reshape(ZL, own, half)
    kern_z = jnp.pad(mine[ZL * own, : ZL * own].reshape(ZL, 1, own), ((0, 0), (0, 7), (0, half - own)))
    ring = jnp.concatenate([gram_z, kern_z], axis=1)
    ring = jnp.broadcast_to(ring[None], (ZH,) + ring.shape).reshape(ZH * ZL, own + 8, half)
    ring = jnp.sum(lax.all_to_all(ring, RING, 0, 0), axis=0)
    both = lax.all_gather(ring, "core", axis=0)
    gram_out = jnp.concatenate([both[0, :own], both[1, :own]], axis=1) / total_rows
    kern_mean = (both[0, own, :own] + both[1, own, :own]) / total_rows
    t_own = land_treat.astype(jnp.float32)
    moment = (jnp.exp(-0.5 * jnp.square(1.0 - t_own)) - jnp.exp(-0.5 * jnp.square(t_own))) * kern_mean
    return gram_out, moment


def solution(mesh):
    fine = Mesh(mesh.devices.reshape(Y, X, ZL, ZH, CORE), ("y", "x", "zl", "zh", "core"))
    rows, rep = ("y", "x", "zl"), ("zh", "core")
    in_specs = (P(rows + rep, None), P(rows + rep), P(rows, None), P(rows))
    out_specs = (P(rows, None), P(rows))
    return jax.shard_map(
        on_device, mesh=fine, in_specs=in_specs, out_specs=out_specs, check_vma=False
    )
```

time: 2150 us -> 98.6 us (0.05)
  blocking collectives: 1530 us -> 42.4 us
  waiting for transfers between devices: 584 us -> 16.3 us
  starting transfers between devices: 0.04 us -> 25.3 us
    unnamed x2 -> x0, blocking collectives: 941 us -> none
    reduce_scatter x1 -> x0, waiting for transfers between devices: 584 us -> none  [on_device(): lax.psum_scatter(gram_term, 'rows', scatter_dimension=0, tiled=True)]
    all_gather x1, blocking collectives: 457 us -> 8.36 us  [on_device(): both = lax.all_gather(ring, 'core', axis=0)]
    psum x1 -> x0, blocking collectives: 134 us -> none  [on_device(): gram_out, moment_out = lax.psum((shares[0], shares[1]), 'rep')]
    all_to_all x0 -> x2, blocking collectives: none -> 34 us  [the longest x1 20 us: on_device(): ring = jnp.sum(lax.all_to_all(ring, RING, 0, 0), axis=0)]
  transfers between devices with their start and end apart: 1 -> 3, of which waited for: 1 -> 3; matrix products, arithmetic and copies ran while one was open for 0% -> 2% of each run, Pallas kernels for 0% -> 0%
where the time goes in v1:
time: 98.6 us; the launch traced here: 98.1 us
  blocking collectives  42.4 us (43%)
  starting transfers between devices  25.3 us (26%)
  waiting for transfers between devices  16.3 us (17%)
  matrix products  6.38 us (6%)
  other arithmetic  4.49 us (5%)
  local copies, waits for them, and re-layouts  2.45 us (2%)
    all_to_all x1, blocking collectives, on_device(): ring = jnp.sum(lax.all_to_all(ring, RING, 0, 0), axis=0)  20 us
    all_to_all x2, starting transfers between devices, spread(): return lax.all_to_all(copies, axes, 0, 0)  19.8 us
    all_to_all x2, waiting for transfers between devices, spread(): return lax.all_to_all(copies, axes, 0, 0)  15.1 us
    all_to_all x1, blocking collectives, on_device(): lax.all_to_all(jnp.concatenate([pair, kern_sum], axis=1), PLANE, 0, 0)  14 us
    all_gather x1, blocking collectives, on_device(): both = lax.all_gather(ring, 'core', axis=0)  8.36 us
    ppermute x1, starting transfers between devices, on_device(): got = lax.ppermute(send, 'core', [(0, 1), (1, 0)])  5.46 us
    dot_general x2, matrix products, on_device(): lax.dot_general(covariates, block, (((1,), (1,)), ((), ())), preferred_el...  3.54 us
    dot_general x2, matrix products, on_device(): lax.dot_general(features, features, (((0,), (0,)), ((), ())), preferred_e...  2.85 us
  transfers between devices with their start and end apart: 3, of which 3 were waited for; matrix products, arithmetic and copies ran while one was open for 2% of the time, Pallas kernels for 0%

profile of v1, /device:TPU:1, one launch (start us, length us, event | category | flops | bytes accessed | tf_op | source)
XLA Modules:
  0.0 98.1 jit_solution(17184891928004220112)
XLA Ops:
  0.6 0.7 fusion.23
  1.3 0.6 broadcast_in_dim.64
  1.9 13.1 %all-to-all-start = ((bf16[8,16,128]{2,1,0:T(8,128)(2,1)}), bf16[8,16,128]{2,1,0:T(8,128)(2,1)S(1)}, u32[]{:S(2)}, u32[]{:S(2)}) async-start(bf16[8,16,128]{2,1,0:T(8,128)(2,1)} %broadcast_in_dim.64), calls=%async_computation | async-start | bytes 65536 | tf_op jit(solution)/shard_map/all_to_all | solution.py:16
  15.0 0.7 broadcast_compare_fusion
  15.7 8.8 %all-to-all-done = bf16[8,16,128]{2,1,0:T(8,128)(2,1)S(1)} async-done(((bf16[8,16,128]{2,1,0:T(8,128)(2,1)}), bf16[8,16,128]{2,1,0:T(8,128)(2,1)S(1)}, u32[]{:S(2)}, u32[]{:S(2)}) %all-to-all-start) | async-done | bytes 32800 | tf_op jit(solution)/shard_map/all_to_all | solution.py:16
  24.5 0.1 reshape_squeeze.7
  24.6 0.7 broadcast_in_dim.65
  25.4 6.8 %all-to-all-start.1 = ((bf16[16,72,128]{2,1,0:T(8,128)(2,1)}), bf16[16,72,128]{2,1,0:T(8,128)(2,1)S(1)}, u32[]{:S(2)}, u32[]{:S(2)}) async-start(bf16[16,72,128]{2,1,0:T(8,128)(2,1)} %broadcast_in_dim.65), calls=%async_computation.1 | async-start | bytes 589824 | tf_op jit(solution)/shard_map/all_to_all | solution.py:16
  32.1 1.4 %multiply_reduce_fusion = f32[2048]{0:T(1024)S(1)} fusion(bf16[2048,128]{1,0:T(8,128)(2,1)} %param.6), kind=kLoop, calls=%fused_computation.21 | loop fusion | flops 784384 | bytes 532480 | tf_op jit(solution)/shard_map/reduce_sum | solution.py:33
  33.6 6.3 %all-to-all-done.1 = bf16[16,72,128]{2,1,0:T(8,128)(2,1)S(1)} async-done(((bf16[16,72,128]{2,1,0:T(8,128)(2,1)}), bf16[16,72,128]{2,1,0:T(8,128)(2,1)S(1)}, u32[]{:S(2)}, u32[]{:S(2)}) %all-to-all-start.1) | async-done | bytes 294944 | tf_op jit(solution)/shard_map/all_to_all | solution.py:16
  39.9 0.2 multiply_reduce_fusion.1
  40.6 2.3 %fusion.29 = (bf16[512]{0:T(512)(128)(2,1)S(1)}, f32[2048,512]{0,1:T(8,128)S(1)}) fusion(bf16[512,128]{1,0:T(8,128)(2,1)S(1)} %bitcast.44, bf16[2048,128]{1,0:T(8,128)(2,1)} %param.6, f32[512]{0:T(512)S(1)} %sub.61, f32[2048]{0:T(1024)S(1)} %broadcast_subtract_fusion), kind=kOutput, calls=%fused_computation.61 | convolution fusion | flops 273677824 | bytes 4860928 | tf_op jit(solution)/shard_map/dot_general | solution.py:47
  42.9 1.4 %fusion.5 = f32[512,512]{1,0:T(8,128)S(1)} fusion(f32[2048,512]{0,1:T(8,128)S(1)} %get-tuple-element.27, f32[512]{0:T(512)S(1)} %slice.101, f32[512]{0:T(512)S(1)} %reshape.123, pred[2048]{0:T(1024)(128)(4,1)S(1)} %broadcast_compare_fusion), kind=kOutput, calls=%fused_computation.9 | convolution fusion | flops 1076887552 | bytes 5249024 | tf_op jit(solution)/shard_map/dot_general | solution.py:60
  44.4 1.2 %fusion.30 = (bf16[512]{0:T(512)(128)(2,1)S(1)}, f32[2048,512]{0,1:T(8,128)S(1)}) fusion(bf16[512,128]{1,0:T(8,128)(2,1)S(1)} %bitcast.43, bf16[2048,128]{1,0:T(8,128)(2,1)S(1)} %copy-done, f32[512]{0:T(512)S(1)} %sub.56, f32[2048]{0:T(1024)S(1)} %broadcast_subtract_fusion), kind=kOutput, calls=%fused_computation.62 | convolution fusion | flops 273677824 | bytes 4860928 | tf_op jit(solution)/shard_map/dot_general | solution.py:47
  45.6 1.4 %fusion.4 = f32[512,512]{1,0:T(8,128)S(1)} fusion(f32[2048,512]{0,1:T(8,128)S(1)} %get-tuple-element.29, f32[512]{0:T(512)S(1)} %slice.95, f32[512]{0:T(512)S(1)} %reshape.122, pred[2048]{0:T(1024)(128)(4,1)S(1)} %broadcast_compare_fusion), kind=kOutput, calls=%fused_computation.8 | convolution fusion | flops 1076887552 | bytes 5249024 | tf_op jit(solution)/shard_map/dot_general | solution.py:60
  47.2 5.5 %collective-permute-start = (bf16[1024,256]{1,0:T(8,128)(2,1)S(1)}, bf16[1024,256]{1,0:T(8,128)(2,1)S(1)}, u32[]{:S(2)}, u32[]{:S(2)}) collective-permute-start(bf16[1024,256]{1,0:T(8,128)(2,1)S(1)} %pad_maximum_fusion), channel_id=1, source_target_pairs={{0,1},{1,0},{2,3},{3,2},{4,5},{5,4},{6,7},{7,6},{8,9},{9,8},{10,11... | collective-permute-start | bytes 1572872 | tf_op jit(solution)/shard_map/ppermute | solution.py:68
  52.6 0.1 concatenate.44
  52.9 1.2 %collective-permute-done = bf16[1024,256]{1,0:T(8,128)(2,1)S(1)} collective-permute-done((bf16[1024,256]{1,0:T(8,128)(2,1)S(1)}, bf16[1024,256]{1,0:T(8,128)(2,1)S(1)}, u32[]{:S(2)}, u32[]{:S(2)}) %collective-permute-start) | collective-permute-done | bytes 524320 | tf_op jit(solution)/shard_map/ppermute | solution.py:68
  54.1 0.1 fusion.13
  54.3 14.0 %all_to_all.20 = bf16[16,72,256]{2,1,0:T(8,128)(2,1)S(1)} all-to-all(bf16[16,72,256]{2,1,0:T(8,128)(2,1)S(1)} %fusion.14), channel_id=1, replica_groups=mesh['y'=4,'x'=4,'zl'=8,'zh'=2,'core'=2] {'y','x'}, dimensions={0} | all-to-all | bytes 1179648 | tf_op jit(solution)/shard_map/all_to_all | solution.py:72
  68.6 20.0 %all_to_all.21 = f32[16,16,256]{2,1,0:T(8,128)S(1)} all-to-all(f32[16,16,256]{2,1,0:T(8,128)S(1)} %bitcast.42), channel_id=1, replica_groups=mesh['y'=4,'x'=4,'zl'=8,'zh'=2,'core'=2] {'zh','zl'}, dimensions={0} | all-to-all | bytes 524288 | tf_op jit(solution)/shard_map/all_to_all | solution.py:78
  88.6 8.4 %all-gather = f32[32,256]{1,0:T(8,128)S(1)} all-gather(f32[16,256]{1,0:T(8,128)S(1)} %reduce_sum.59), channel_id=2, replica_groups=mesh['y'=4,'x'=4,'zl'=8,'zh'=2,'core'=2] {'core'}, dimensions={0}, use_global_device_ids=true | all-gather | bytes 49152 | tf_op jit(solution)/shard_map/all_gather | solution.py:79
  97.0 0.5 bitcast_multiply_fusion
  97.5 0.6 maximum_multiply_fusion
  (36 shorter events, 1.2 us)
Async XLA Ops:
  1.9 22.6 %all-to-all-start = ((bf16[8,16,128]{2,1,0:T(8,128)(2,1)}), bf16[8,16,128]{2,1,0:T(8,128)(2,1)S(1)}, u32[]{:S(2)}, u32[]{:S(2)}) async-start(bf16[8,16,128]{2,1,0:T(8,128)(2,1)} %broadcast_in_dim.64), calls=%async_computation | async-start | bytes 65536 | tf_op jit(solution)/shard_map/all_to_all | solution.py:16
  25.4 14.5 %all-to-all-start.1 = ((bf16[16,72,128]{2,1,0:T(8,128)(2,1)}), bf16[16,72,128]{2,1,0:T(8,128)(2,1)S(1)}, u32[]{:S(2)}, u32[]{:S(2)}) async-start(bf16[16,72,128]{2,1,0:T(8,128)(2,1)} %broadcast_in_dim.65), calls=%async_computation.1 | async-start | bytes 589824 | tf_op jit(solution)/shard_map/all_to_all | solution.py:16
  42.9 1.5 %copy-start = (bf16[2048,128]{1,0:T(8,128)(2,1)S(1)}, bf16[2048,128]{1,0:T(8,128)(2,1)}, u32[]{:S(2)}) copy-start(bf16[2048,128]{1,0:T(8,128)(2,1)} %param.6) | copy-start | bytes 1572868
  47.2 7.0 %collective-permute-start = (bf16[1024,256]{1,0:T(8,128)(2,1)S(1)}, bf16[1024,256]{1,0:T(8,128)(2,1)S(1)}, u32[]{:S(2)}, u32[]{:S(2)}) collective-permute-start(bf16[1024,256]{1,0:T(8,128)(2,1)S(1)} %pad_maximum_fusion), channel_id=1, source_target_pairs={{0,1},{1,0},{2,3},{3,2},{4,5},{5,4},{6,7},{7,6},{8,9},{9,8},{10,11... | collective-permute-start | bytes 1572872 | tf_op jit(solution)/shard_map/ppermute | solution.py:68
  52.8 44.1 %copy-start.1 = (bf16[8]{0:T(256)(128)(2,1)S(1)}, bf16[8]{0:T(256)(128)(2,1)}, u32[]{:S(2)}) copy-start(bf16[8]{0:T(256)(128)(2,1)} %param.9) | copy-start | bytes 52

commit v2 on v1

v2 whole, which is shorter than its diff:
```python
import jax
import jax.numpy as jnp
from jax import lax
from jax.experimental import pallas as pl
from jax.experimental.pallas import tpu as pltpu
from jax.sharding import Mesh, PartitionSpec as P

Y, X, ZL, ZH, CORE = 4, 4, 8, 2, 2
PLANE = ("y", "x")
RING = ("zh", "zl")
PANELS = 2
MASKS = 16
BLOCK = 512
GROUP = 16
LANES = 128

gamma_rate = 0.03125


def spread(block, axes, count):
    copies = jnp.broadcast_to(block[None], (count,) + block.shape)
    return lax.all_to_all(copies, axes, 0, 0)


def three_parts(value):
    high = lax.reduce_precision(value, 8, 7)
    rest = value - high
    middle = lax.reduce_precision(rest, 8, 7)
    return high, middle, rest - middle


def by_lane(shape, offset, columns):
    lane = lax.broadcasted_iota(jnp.int32, shape, 1) - offset
    out = jnp.zeros(shape, jnp.float32)
    for at, column in enumerate(columns):
        out = jnp.where(lane == at, column, out)
    return out.astype(jnp.bfloat16)


def row_side(covariates, treated):
    width = covariates.shape[1]
    rows_f = covariates.astype(jnp.float32)
    flag = treated.astype(jnp.float32)
    own = gamma_rate * (2.0 * width - jnp.sum(rows_f * rows_f, axis=1)) - 0.5 * flag
    parts = [part[:, None] for part in three_parts(own)]
    extra = by_lane((covariates.shape[0], LANES), 0, parts + [flag[:, None], 1.0, 1.0, 1.0])
    return jnp.concatenate([covariates, extra], axis=1)


def land_side(landmarks, land_treat):
    land_f = landmarks.astype(jnp.float32)
    value = land_treat.astype(jnp.float32)
    own = -gamma_rate * jnp.sum(land_f * land_f, axis=1) - 0.5 * jnp.square(value)
    parts = [part[:, None] for part in three_parts(own)]
    offset = GROUP * lax.axis_index("zl")
    extra = by_lane((landmarks.shape[0], LANES), offset, [1.0, 1.0, 1.0, value[:, None]] + parts)
    scaled = (land_f * (2.0 * gamma_rate)).astype(jnp.bfloat16)
    return jnp.concatenate([scaled, extra], axis=0)


def gram_kernel(core_ref, own_ref, other_ref, plane_ref, out_ref, land, feat, acc):
    step = pl.program_id(0)
    count = pl.num_programs(0)
    core = core_ref[0]
    places, place_rows = plane_ref.shape[0], plane_ref.shape[1] - 8
    size = places * place_rows // PANELS
    half = size // CORE
    per_panel = places // PANELS

    @pl.when(step == 0)
    def _():
        lane = lax.broadcasted_iota(jnp.int32, (8, LANES), 1)
        for place in range(places):
            base = (place // per_panel) * (size + MASKS) + (place % per_panel) * place_rows
            land[base : base + place_rows, :LANES] = plane_ref[place, :place_rows]
            packed = plane_ref[place, place_rows:].astype(jnp.float32)
            pieces = []
            for group in range(place_rows // 8):
                rolled = packed if group == 0 else pltpu.roll(packed, LANES - GROUP * group, 1)
                pieces.append(jnp.where(lane < GROUP, rolled, 0.0))
            extra = jnp.concatenate(pieces, axis=0)
            land[base : base + place_rows, LANES:] = extra.astype(jnp.bfloat16)
        lane = lax.broadcasted_iota(jnp.int32, (MASKS, LANES), 1)
        row = lax.broadcasted_iota(jnp.int32, (MASKS, LANES), 0)
        flag = jnp.where(lane == 3, 1.0, 0.0)
        other = jnp.where(lane == 4, 1.0, 0.0) - flag
        mask = jnp.where(row == 0, flag, jnp.where(row == 1, other, 0.0)).astype(jnp.bfloat16)
        for panel in range(PANELS):
            base = panel * (size + MASKS) + size
            land[base : base + MASKS, :LANES] = jnp.zeros((MASKS, LANES), jnp.bfloat16)
            land[base : base + MASKS, LANES:] = mask
        acc[...] = jnp.zeros_like(acc)

    def work(rows_ref):
        for panel in range(PANELS):
            base = panel * (size + MASKS)
            arg = lax.dot_general(
                land[base : base + size + MASKS, :],
                rows_ref[...],
                (((1,), (1,)), ((), ())),
                preferred_element_type=jnp.float32,
            )
            feat[panel, :size, :] = jnp.exp(arg[:size]).astype(jnp.bfloat16)
            feat[panel, size:, :] = arg[size:].astype(jnp.bfloat16)
        for panel in range(PANELS):
            mine = feat[panel, pl.ds(pl.multiple_of(core * half, half), half), :]
            acc[panel] += lax.dot_general(
                feat[panel], mine, (((1,), (1,)), ((), ())), preferred_element_type=jnp.float32
            )

    @pl.when(step < count // 2)
    def _():
        work(own_ref)

    @pl.when(step >= count // 2)
    def _():
        work(other_ref)

    @pl.when(step == count - 1)
    def _():
        for place in range(places):
            panel, spot = place // per_panel, place % per_panel
            first = spot * place_rows
            for tile in range(half // LANES):
                out_ref[place, tile * place_rows : (tile + 1) * place_rows, :] = acc[
                    panel, first : first + place_rows, tile * LANES : (tile + 1) * LANES
                ].astype(jnp.bfloat16)
            at = (first % half) // LANES * LANES
            sums = acc[panel, size : size + 8, at : at + LANES]
            sums = jnp.where(core == first // half, sums, 0.0)
            out_ref[place, half // LANES * place_rows :, :] = sums.astype(jnp.bfloat16)


def chip_gram(core, own, other, plane):
    places, place_rows = plane.shape[0], plane.shape[1] - 8
    size = places * place_rows // PANELS
    half = size // CORE
    steps = own.shape[0] // BLOCK
    out_rows = half // LANES * place_rows + 8
    grid_spec = pltpu.PrefetchScalarGridSpec(
        num_scalar_prefetch=1,
        grid=(2 * steps,),
        in_specs=[
            pl.BlockSpec((BLOCK, own.shape[1]), lambda i, c: (jnp.minimum(i, steps - 1), 0)),
            pl.BlockSpec((BLOCK, own.shape[1]), lambda i, c: (jnp.maximum(i - steps, 0), 0)),
            pl.BlockSpec(plane.shape, lambda i, c: (0, 0, 0)),
        ],
        out_specs=pl.BlockSpec((places, out_rows, LANES), lambda i, c: (0, 0, 0)),
        scratch_shapes=[
            pltpu.VMEM((PANELS * (size + MASKS), 2 * LANES), jnp.bfloat16),
            pltpu.VMEM((PANELS, size + MASKS, BLOCK), jnp.bfloat16),
            pltpu.VMEM((PANELS, size + MASKS, half), jnp.float32),
        ],
    )
    rows = 2 * own.shape[0]
    flops = 2 * rows * PANELS * size * (2 * LANES + half)
    return pl.pallas_call(
        gram_kernel,
        grid_spec=grid_spec,
        out_shape=jax.ShapeDtypeStruct((places, out_rows, LANES), jnp.bfloat16),
        compiler_params=pltpu.CompilerParams(
            dimension_semantics=("arbitrary",), vmem_limit_bytes=48 << 20
        ),
        cost_estimate=pl.CostEstimate(
            flops=flops, transcendentals=rows * PANELS * size, bytes_accessed=4 << 20
        ),
        name="chip_gram",
    )(core, own, other, plane)


def on_device(covariates, treated, landmarks, land_treat):
    width = covariates.shape[1]
    total_rows = covariates.shape[0] * Y * X * ZL * ZH * CORE
    own = landmarks.shape[0]
    run = spread(land_side(landmarks, land_treat), "zl", ZL)
    extra = jnp.sum(run[:, own:].astype(jnp.float32), axis=0).astype(jnp.bfloat16)
    run = jnp.concatenate([run[:, :own].reshape(ZL * own, width), extra], axis=0)
    plane = spread(run, PLANE, Y * X)

    rows_own = row_side(covariates, treated)
    rows_other = lax.ppermute(rows_own, "core", [(0, 1), (1, 0)])
    core = lax.axis_index("core").astype(jnp.int32).reshape(1)
    terms = chip_gram(core, rows_own, rows_other, plane)

    mine = lax.all_to_all(terms, PLANE, 0, 0)
    mine = jnp.sum(mine.astype(jnp.float32), axis=0)
    tiles = (mine.shape[0] - 8) // (ZL * own)
    gram_z = mine[: tiles * ZL * own].reshape(tiles, ZL, own, LANES).transpose(1, 0, 2, 3)
    sums_z = jnp.broadcast_to(mine[None, tiles * ZL * own :], (ZL, 8, LANES))
    ring = jnp.concatenate([gram_z.reshape(ZL, tiles * own, LANES), sums_z], axis=1)
    ring = jnp.broadcast_to(ring[None], (ZH,) + ring.shape).reshape((ZH * ZL,) + ring.shape[1:])
    ring = jnp.sum(lax.all_to_all(ring, RING, 0, 0), axis=0)
    both = lax.all_gather(ring, "core", axis=0)
    gram = both[:, : tiles * own].reshape(CORE * tiles, own, LANES).transpose(1, 0, 2)
    gram_out = gram.reshape(own, CORE * tiles * LANES) * (1.0 / total_rows)
    sums = both[0, tiles * own : tiles * own + 2] + both[1, tiles * own : tiles * own + 2]
    at = 64 * (lax.axis_index("x") % 2) + own * lax.axis_index("zl")
    sums = lax.dynamic_slice(sums, (0, at), (2, own))
    t_own = land_treat.astype(jnp.float32)
    on_one = jnp.exp(-0.5 * jnp.square(1.0 - t_own))
    on_zero = jnp.exp(-0.5 * jnp.square(t_own))
    moment = (on_one - on_zero) * ((sums[0] / on_one + sums[1] / on_zero) * (1.0 / total_rows))
    return gram_out, moment


def solution(mesh):
    fine = Mesh(mesh.devices.reshape(Y, X, ZL, ZH, CORE), ("y", "x", "zl", "zh", "core"))
    rows, rep = ("y", "x", "zl"), ("zh", "core")
    in_specs = (P(rows + rep, None), P(rows + rep), P(rows, None), P(rows))
    out_specs = (P(rows, None), P(rows))
    return jax.shard_map(
        on_device, mesh=fine, in_specs=in_specs, out_specs=out_specs, check_vma=False
    )
```

time: 98.6 us -> 96.7 us (0.981)
  Pallas kernels: 0 us -> 8.09 us
  matrix products: 6.38 us -> 0 us
  blocking collectives: 42.4 us -> 36.2 us
  waiting for transfers between devices: 16.3 us -> 20 us
  starting transfers between devices: 25.3 us -> 23 us
  other arithmetic: 4.49 us -> 6.42 us
    all_to_all x2 -> x1, starting transfers between devices: 19.8 us -> 6.75 us  [spread(): return lax.all_to_all(copies, axes, 0, 0)]
    all_to_all x0 -> x1, waiting for transfers between devices: none -> 12.3 us  [on_device(): ring = jnp.sum(lax.all_to_all(ring, RING, 0, 0), axis=0)]
    pallas_call x0 -> x1, Pallas kernels: none -> 8.09 us  [chip_gram(): pl.pallas_call(gram_kernel, grid_spec=grid_spec, out_shape=jax.ShapeDtype...]
    all_to_all x0 -> x1, starting transfers between devices: none -> 7.42 us  [on_device(): ring = jnp.sum(lax.all_to_all(ring, RING, 0, 0), axis=0)]
    all_to_all x2 -> x1, waiting for transfers between devices: 15.1 us -> 7.73 us  [spread(): return lax.all_to_all(copies, axes, 0, 0)]
    dot_general x4 -> x0, matrix products: 6.38 us -> none  [the longest x2 3.54 us: on_device(): lax.dot_general(covariates, block, (((1,), (1,)), ((), ())), preferred_el...]
    all_to_all x2, blocking collectives: 34 us -> 28.7 us  [the longest x1 16.2 us: spread(): return lax.all_to_all(copies, axes, 0, 0)]
    ppermute x1, starting transfers between devices: 5.46 us -> 8.79 us  [on_device(): rows_other = lax.ppermute(rows_own, 'core', [(0, 1), (1, 0)])]
  transfers between devices with their start and end apart: 3 -> 3, of which waited for: 3 -> 2; matrix products, arithmetic and copies ran while one was open for 2% -> 1% of each run, Pallas kernels for 0% -> 0%
where the time goes in v2:
time: 96.7 us; the launch traced here: 96.2 us
  blocking collectives  36.2 us (37%)
  starting transfers between devices  23 us (24%)
  waiting for transfers between devices  20 us (21%)
  Pallas kernels  8.09 us (8%)
  other arithmetic  6.42 us (7%)
  local copies, waits for them, and re-layouts  1.56 us (2%)
    all_to_all x1, blocking collectives, spread(): return lax.all_to_all(copies, axes, 0, 0)  16.2 us
    all_to_all x1, blocking collectives, on_device(): mine = lax.all_to_all(terms, PLANE, 0, 0)  12.5 us
    all_to_all x1, waiting for transfers between devices, on_device(): ring = jnp.sum(lax.all_to_all(ring, RING, 0, 0), axis=0)  12.3 us
    ppermute x1, starting transfers between devices, on_device(): rows_other = lax.ppermute(rows_own, 'core', [(0, 1), (1, 0)])  8.79 us
    pallas_call x1, Pallas kernels, chip_gram(): pl.pallas_call(gram_kernel, grid_spec=grid_spec, out_shape=jax.ShapeDtype...  8.09 us
    all_to_all x1, waiting for transfers between devices, spread(): return lax.all_to_all(copies, axes, 0, 0)  7.73 us
    all_gather x1, blocking collectives, on_device(): both = lax.all_gather(ring, 'core', axis=0)  7.55 us
    all_to_all x1, starting transfers between devices, on_device(): ring = jnp.sum(lax.all_to_all(ring, RING, 0, 0), axis=0)  7.42 us
  transfers between devices with their start and end apart: 3, of which 2 were waited for; matrix products, arithmetic and copies ran while one was open for 1% of the time, Pallas kernels for 0%

profile of v2, /device:TPU:1, one launch (start us, length us, event | category | flops | bytes accessed | tf_op | source)
XLA Modules:
  0.0 96.2 jit_solution(10111700345017734941)
XLA Ops:
  0.6 0.0 copy-start
  0.7 0.8 convert_element_type.27
  1.4 1.4 %multiply_reduce_fusion = f32[2048]{0:T(1024)S(1)} fusion(bf16[2048,128]{1,0:T(8,128)(2,1)} %param.4), kind=kLoop, calls=%fused_computation.3 | loop fusion | flops 784384 | bytes 532480 | tf_op jit(solution)/shard_map/reduce_sum | solution.py:44
  2.8 0.7 reduce-precision_subtract_fusion
  3.5 1.9 %select_convert_fusion = bf16[2048,128]{1,0:T(8,128)(2,1)S(1)} fusion(bf16[2048]{0:T(1024)(128)(2,1)S(1)} %get-tuple-element.8, bf16[2048]{0:T(1024)(128)(2,1)S(1)} %get-tuple-element.7, bf16[2048]{0:T(1024)(128)(2,1)S(1)} %get-tuple-element.6, bf16[2048]{0:T(1024)(128)(2,1)S(1)} %convert_element_type.27, pred[128]{0:T(512)(128)(4,1)S(1)} %get-tuple-element.13, ...), kind=kLoop, calls=%fused_computation.2 | loop fusion | flops 1835008 | bytes 541568 | tf_op jit(solution)/shard_map/convert_element_type | solution.py:37
  5.5 0.0 copy-start.2
  5.5 0.1 pad_maximum_fusion.own_ref
  5.6 8.8 %collective-permute-start = (bf16[2048,256]{1,0:T(8,128)(2,1)S(1)}, bf16[2048,256]{1,0:T(8,128)(2,1)S(1)}, u32[]{:S(2)}, u32[]{:S(2)}) collective-permute-start(bf16[2048,256]{1,0:T(8,128)(2,1)S(1)} %pad_maximum_fusion.own_ref), channel_id=1, source_target_pairs={{0,1},{1,0},{2,3},{3,2},{4,5},{5,4},{6,7},{7,6},{8,9},{9,8},{10,11... | collective-permute-start | bytes 3145736 | tf_op jit(solution)/shard_map/ppermute | solution.py:181
  14.5 0.1 fusion
  14.6 0.1 select_convert_fusion.1
  14.7 16.2 %all_to_all.20 = bf16[8,16,128]{2,1,0:T(8,128)(2,1)S(1)} all-to-all(bf16[8,16,128]{2,1,0:T(8,128)(2,1)S(1)} %broadcast_in_dim.111), channel_id=1, replica_groups=mesh['y'=4,'x'=4,'zl'=8,'zh'=2,'core'=2] {'zl'}, dimensions={0} | all-to-all | bytes 65536 | tf_op jit(solution)/shard_map/all_to_all | solution.py:22
  31.0 0.7 broadcast_in_dim.112
  31.7 6.8 %all-to-all-start.1 = ((bf16[16,72,128]{2,1,0:T(8,128)(2,1)}), bf16[16,72,128]{2,1,0:T(8,128)(2,1)S(1)}, u32[]{:S(2)}, u32[]{:S(2)}) async-start(bf16[16,72,128]{2,1,0:T(8,128)(2,1)} %broadcast_in_dim.112), calls=%async_computation.1 | async-start | bytes 589824 | tf_op jit(solution)/shard_map/all_to_all | solution.py:22
  38.5 7.7 %all-to-all-done.1.plane_ref = bf16[16,72,128]{2,1,0:T(8,128)(2,1)S(1)} async-done(((bf16[16,72,128]{2,1,0:T(8,128)(2,1)}), bf16[16,72,128]{2,1,0:T(8,128)(2,1)S(1)}, u32[]{:S(2)}, u32[]{:S(2)}) %all-to-all-start.1) | async-done | bytes 294944 | tf_op jit(solution)/shard_map/all_to_all | solution.py:22
  46.2 8.1 %chip_gram.1 = bf16[16,136,128]{2,1,0:T(8,128)(2,1)S(1)} custom-call(s32[1]{0:T(128)} %bitcast.core_ref, bf16[2048,256]{1,0:T(8,128)(2,1)S(1)} %pad_maximum_fusion.own_ref, bf16[2048,256]{1,0:T(8,128)(2,1)S(1)} %collective-permute-done.other_ref, bf16[16,72,128]{2,1,0:T(8,128)(2,1)S(1)} %all-to-all-done.1.plane_ref), custom_call_target="tpu_custom_call" | custom-call | flops 4294967296 | bytes 4194304 | tf_op jit(solution)/shard_map/chip_gram/pallas_call | solution.py:157
  54.3 12.5 %all_to_all.21 = bf16[16,136,128]{2,1,0:T(8,128)(2,1)S(1)} all-to-all(bf16[16,136,128]{2,1,0:T(8,128)(2,1)S(1)} %chip_gram.1), channel_id=1, replica_groups=mesh['y'=4,'x'=4,'zl'=8,'zh'=2,'core'=2] {'y','x'}, dimensions={0} | all-to-all | bytes 1114112 | tf_op jit(solution)/shard_map/all_to_all | solution.py:185
  66.8 0.1 convert_reduce_fusion
  66.9 0.7 broadcast_in_dim.114
  67.6 7.4 %all-to-all-start.3 = ((f32[16,24,128]{2,1,0:T(8,128)}), f32[16,24,128]{2,1,0:T(8,128)S(1)}, u32[]{:S(2)}, u32[]{:S(2)}) async-start(f32[16,24,128]{2,1,0:T(8,128)} %bitcast.5), calls=%async_computation.3 | async-start | bytes 393216 | tf_op jit(solution)/shard_map/all_to_all | solution.py:192
  75.1 12.3 %all-to-all-done.3 = f32[16,24,128]{2,1,0:T(8,128)S(1)} async-done(((f32[16,24,128]{2,1,0:T(8,128)}), f32[16,24,128]{2,1,0:T(8,128)S(1)}, u32[]{:S(2)}, u32[]{:S(2)}) %all-to-all-start.3) | async-done | bytes 196640 | tf_op jit(solution)/shard_map/all_to_all | solution.py:192
  87.4 7.6 %all-gather = f32[48,128]{1,0:T(8,128)S(1)} all-gather(f32[24,128]{1,0:T(8,128)S(1)} %reduce_sum.52), channel_id=2, replica_groups=mesh['y'=4,'x'=4,'zl'=8,'zh'=2,'core'=2] {'core'}, dimensions={0}, use_global_device_ids=true | all-gather | bytes 36864 | tf_op jit(solution)/shard_map/all_gather | solution.py:193
  95.0 0.6 slice_multiply_fusion
  95.6 0.1 constant_dynamic-slice_fusion
  95.7 0.5 multiply_multiply_fusion
  (26 shorter events, 0.2 us)
Async XLA Ops:
  0.6 4.8 %copy-start = (bf16[2048,128]{1,0:T(8,128)(2,1)S(1)}, bf16[2048,128]{1,0:T(8,128)(2,1)}, u32[]{:S(2)}) copy-start(bf16[2048,128]{1,0:T(8,128)(2,1)} %param.4) | copy-start | bytes 1572868
  5.5 9.0 %copy-start.2 = (bf16[8,128]{1,0:T(8,128)(2,1)S(1)}, bf16[8,128]{1,0:T(8,128)(2,1)}, u32[]{:S(2)}) copy-start(bf16[8,128]{1,0:T(8,128)(2,1)} %param.6) | copy-start | bytes 6148
  5.5 9.1 %copy-start.1 = (bf16[8]{0:T(256)(128)(2,1)S(1)}, bf16[8]{0:T(256)(128)(2,1)}, u32[]{:S(2)}) copy-start(bf16[8]{0:T(256)(128)(2,1)} %param.7) | copy-start | bytes 52
  5.6 40.6 %collective-permute-start = (bf16[2048,256]{1,0:T(8,128)(2,1)S(1)}, bf16[2048,256]{1,0:T(8,128)(2,1)S(1)}, u32[]{:S(2)}, u32[]{:S(2)}) collective-permute-start(bf16[2048,256]{1,0:T(8,128)(2,1)S(1)} %pad_maximum_fusion.own_ref), channel_id=1, source_target_pairs={{0,1},{1,0},{2,3},{3,2},{4,5},{5,4},{6,7},{7,6},{8,9},{9,8},{10,11... | collective-permute-start | bytes 3145736 | tf_op jit(solution)/shard_map/ppermute | solution.py:181
  31.7 14.5 %all-to-all-start.1 = ((bf16[16,72,128]{2,1,0:T(8,128)(2,1)}), bf16[16,72,128]{2,1,0:T(8,128)(2,1)S(1)}, u32[]{:S(2)}, u32[]{:S(2)}) async-start(bf16[16,72,128]{2,1,0:T(8,128)(2,1)} %broadcast_in_dim.112), calls=%async_computation.1 | async-start | bytes 589824 | tf_op jit(solution)/shard_map/all_to_all | solution.py:22
  67.6 19.8 %all-to-all-start.3 = ((f32[16,24,128]{2,1,0:T(8,128)}), f32[16,24,128]{2,1,0:T(8,128)S(1)}, u32[]{:S(2)}, u32[]{:S(2)}) async-start(f32[16,24,128]{2,1,0:T(8,128)} %bitcast.5), calls=%async_computation.3 | async-start | bytes 393216 | tf_op jit(solution)/shard_map/all_to_all | solution.py:192

commit v3 on v0

v3 whole, which is shorter than its diff:
```python
import jax
import jax.numpy as jnp
from jax import lax
from jax.experimental import pallas as pl
from jax.experimental.pallas import tpu as pltpu
from jax.sharding import Mesh, PartitionSpec as P

Y, X, ZL, ZH, CORE = 4, 4, 8, 2, 2
PLANE = ("y", "x")
RING = ("zh", "zl")
PANELS = 2
OWN = 8
RUN = ZL * OWN
MASKS = 16
BLOCK = 1024
GROUP = 16
LANES = 128
NT = (((1,), (1,)), ((), ()))

gamma_rate = 0.03125


def call(kernel, out_shape, *args, scratch=(), cost=None, vmem=16 << 20):
    whole = pl.BlockSpec(memory_space=pltpu.VMEM)
    several = isinstance(out_shape, tuple)
    return pl.pallas_call(
        kernel,
        in_specs=[whole] * len(args),
        out_specs=(whole,) * len(out_shape) if several else whole,
        out_shape=out_shape,
        scratch_shapes=list(scratch),
        compiler_params=pltpu.CompilerParams(vmem_limit_bytes=vmem),
        cost_estimate=cost,
        name=kernel.__name__,
    )(*args)


def rounded(value):
    return value.astype(jnp.bfloat16).astype(jnp.float32)


def three_parts(value):
    high = rounded(value)
    middle = rounded(value - high)
    return high, middle, value - high - middle


def pack_kernel(land_ref, treat_ref, out_ref):
    land = land_ref[...].astype(jnp.float32)
    row = lax.broadcasted_iota(jnp.int32, (OWN, OWN), 0)
    col = lax.broadcasted_iota(jnp.int32, (OWN, OWN), 1)
    treat = jnp.broadcast_to(treat_ref[...].astype(jnp.float32), (OWN, OWN))
    treat = jnp.sum(jnp.where(row == col, treat, 0.0), axis=1, keepdims=True)
    own = -gamma_rate * jnp.sum(land * land, axis=1, keepdims=True) - 0.5 * treat * treat
    lane = lax.broadcasted_iota(jnp.int32, (OWN, LANES), 1) - GROUP * lax.axis_index("zl")
    extra = jnp.where((lane >= 0) & (lane < 3), 1.0, 0.0)
    for at, part in enumerate((treat,) + three_parts(own)):
        extra = jnp.where(lane == 3 + at, part, extra)
    land = (land * (2.0 * gamma_rate)).astype(jnp.bfloat16)
    extra = extra.astype(jnp.bfloat16)
    for place in range(ZL):
        out_ref[place, :OWN] = land
        out_ref[place, OWN:] = extra


def run_kernel(run_ref, out_ref):
    extra = run_ref[0, OWN:].astype(jnp.float32)
    for place in range(1, ZL):
        extra += run_ref[place, OWN:].astype(jnp.float32)
    extra = extra.astype(jnp.bfloat16)
    for place in range(Y * X):
        for part in range(ZL):
            out_ref[place, part * OWN : (part + 1) * OWN] = run_ref[part, :OWN]
        out_ref[place, RUN:] = extra


def gram_kernel(rows_ref, flag_ref, plane_ref, send_ref, keep_ref, land, feat, acc):
    core = lax.axis_index("core")
    per_panel = Y * X // PANELS
    size = per_panel * RUN
    half = size // CORE
    rows, width = rows_ref.shape
    lane = lax.broadcasted_iota(jnp.int32, (8, LANES), 1)
    for place in range(Y * X):
        panel, base = place // per_panel, (place % per_panel) * RUN
        land[panel, base : base + RUN, :LANES] = plane_ref[place, :RUN]
        packed = plane_ref[place, RUN:].astype(jnp.float32)
        pieces = []
        for group in range(ZL):
            rolled = packed if group == 0 else pltpu.roll(packed, LANES - GROUP * group, 1)
            pieces.append(jnp.where(lane < GROUP, rolled, 0.0))
        extra = jnp.concatenate(pieces, axis=0).astype(jnp.bfloat16)
        land[panel, base : base + RUN, LANES:] = extra
    ones = jnp.ones((8, 2 * width), jnp.bfloat16)
    for at in range(0, rows, BLOCK):
        block = rows_ref[at : at + BLOCK, :]
        square = jnp.square(block.astype(jnp.float32))
        high = square.astype(jnp.bfloat16)
        low = (square - high.astype(jnp.float32)).astype(jnp.bfloat16)
        total = lax.dot_general(
            ones, jnp.concatenate([high, low], axis=1), NT, preferred_element_type=jnp.float32
        )
        flag = flag_ref[0:1, at : at + BLOCK].astype(jnp.float32)
        own = three_parts(gamma_rate * (2.0 * width - total) - 0.5 * flag)
        row = lax.broadcasted_iota(jnp.int32, (8, BLOCK), 0)
        extra = jnp.where(row == 3, flag, 1.0)
        for index, part in enumerate(own):
            extra = jnp.where(row == index, part, extra)
        extra = jnp.concatenate([extra, jnp.zeros((LANES - 8, BLOCK), jnp.float32)], axis=0)
        wide = jnp.concatenate([block, extra.T.astype(jnp.bfloat16)], axis=1)
        row = lax.broadcasted_iota(jnp.int32, (MASKS, BLOCK), 0)
        mask = jnp.where(row == 0, flag, jnp.where(row == 1, 1.0 - flag, 0.0))
        for panel in range(PANELS):
            arg = lax.dot_general(land[panel], wide, NT, preferred_element_type=jnp.float32)
            feat[panel, :size, at : at + BLOCK] = jnp.exp(arg).astype(jnp.bfloat16)
            feat[panel, size:, at : at + BLOCK] = mask.astype(jnp.bfloat16)
    for panel in range(PANELS):
        for which, out_ref in ((1 - core, send_ref), (core, keep_ref)):
            mine = feat[panel, pl.ds(pl.multiple_of(which * half, half), half), :]
            acc[...] = lax.dot_general(feat[panel], mine, NT, preferred_element_type=jnp.float32)
            for spot in range(per_panel):
                place, first = panel * per_panel + spot, spot * RUN
                for tile in range(half // LANES):
                    out_ref[place, tile * RUN : (tile + 1) * RUN, :] = acc[
                        first : first + RUN, tile * LANES : (tile + 1) * LANES
                    ].astype(out_ref.dtype)
                lanes = (first % half) // LANES * LANES
                sums = acc[size : size + 8, lanes : lanes + LANES]
                sums = jnp.where(which == first // half, sums, 0.0)
                out_ref[place, half // LANES * RUN :, :] = sums.astype(out_ref.dtype)


def chip_gram(rows, flag, plane):
    size = Y * X // PANELS * RUN
    half = size // CORE
    shape = (Y * X, half // LANES * RUN + 8, LANES)
    count, width = rows.shape
    return call(
        gram_kernel,
        (jax.ShapeDtypeStruct(shape, jnp.bfloat16), jax.ShapeDtypeStruct(shape, jnp.float32)),
        rows,
        flag,
        plane,
        scratch=[
            pltpu.VMEM((PANELS, size, 2 * LANES), jnp.bfloat16),
            pltpu.VMEM((PANELS, size + MASKS, count), jnp.bfloat16),
            pltpu.VMEM((size + MASKS, half), jnp.float32),
        ],
        cost=pl.CostEstimate(
            flops=2 * count * PANELS * size * (size + 2 * width),
            transcendentals=count * PANELS * size,
            bytes_accessed=4 << 20,
        ),
        vmem=40 << 20,
    )


def pair_kernel(keep_ref, got_ref, out_ref):
    out_ref[...] = (keep_ref[...] + got_ref[...].astype(jnp.float32)).astype(jnp.bfloat16)


def plane_sum_kernel(terms_ref, out_ref):
    total = terms_ref[0].astype(jnp.float32)
    for place in range(1, Y * X):
        total += terms_ref[place].astype(jnp.float32)
    total = total.astype(jnp.bfloat16)
    tiles = (total.shape[0] - 8) // RUN
    for high in range(ZH):
        for low in range(ZL):
            for tile in range(tiles):
                at = tile * RUN + low * OWN
                out_ref[high * ZL + low, tile * OWN : (tile + 1) * OWN] = total[at : at + OWN]
            out_ref[high * ZL + low, tiles * OWN :] = total[tiles * RUN :]


def ring_sum_kernel(terms_ref, out_ref):
    total = terms_ref[0].astype(jnp.float32)
    for place in range(1, ZH * ZL):
        total += terms_ref[place].astype(jnp.float32)
    out_ref[...] = total


def finish_kernel(scale, both_ref, treat_ref, gram_ref, moment_ref):
    rows = both_ref.shape[0] // CORE
    tiles = (rows - 8) // OWN
    for core in range(CORE):
        for tile in range(tiles):
            at = core * tiles + tile
            first = core * rows + tile * OWN
            gram_ref[:, at * LANES : (at + 1) * LANES] = both_ref[first : first + OWN] * scale
    sums = both_ref[tiles * OWN : rows] + both_ref[rows + tiles * OWN :]
    at = RUN * (lax.axis_index("x") % (LANES // RUN)) + OWN * lax.axis_index("zl")
    sums = pltpu.roll(sums, (LANES - at) % LANES, 1)
    treat = treat_ref[...].astype(jnp.float32)
    on_one = jnp.exp(-0.5 * jnp.square(1.0 - treat))
    on_zero = jnp.exp(-0.5 * jnp.square(treat))
    kern = sums[0:1, :OWN] / on_one + sums[1:2, :OWN] / on_zero
    moment_ref[...] = (on_one - on_zero) * (kern * scale)


def on_device(covariates, treated, landmarks, land_treat):
    count, width = covariates.shape
    scale = 1.0 / (count * Y * X * ZL * ZH * CORE)
    bf16, f32 = jnp.bfloat16, jnp.float32
    treat_row = land_treat.reshape(1, OWN)
    run = call(pack_kernel, jax.ShapeDtypeStruct((ZL, 2 * OWN, width), bf16), landmarks, treat_row)
    run = lax.all_to_all(run, "zl", 0, 0)
    plane = call(run_kernel, jax.ShapeDtypeStruct((Y * X, RUN + 8, width), bf16), run)
    plane = lax.all_to_all(plane, PLANE, 0, 0)

    send, keep = chip_gram(covariates, treated.reshape(1, count), plane)
    got = lax.ppermute(send, "core", [(0, 1), (1, 0)])
    terms = call(pair_kernel, jax.ShapeDtypeStruct(send.shape, bf16), keep, got)
    terms = lax.all_to_all(terms, PLANE, 0, 0)
    rows = (terms.shape[1] - 8) // ZL + 8
    ring = call(plane_sum_kernel, jax.ShapeDtypeStruct((ZH * ZL, rows, LANES), bf16), terms)
    ring = lax.all_to_all(ring, RING, 0, 0)
    ring = call(ring_sum_kernel, jax.ShapeDtypeStruct((rows, LANES), f32), ring)
    both = lax.all_gather(ring, "core", axis=0, tiled=True)

    def finish(*refs):
        finish_kernel(scale, *refs)

    gram, moment = call(
        finish,
        (
            jax.ShapeDtypeStruct((OWN, CORE * (rows - 8) // OWN * LANES), f32),
            jax.ShapeDtypeStruct((1, OWN), f32),
        ),
        both,
        treat_row,
    )
    return gram, moment.reshape(OWN)


def solution(mesh):
    fine = Mesh(mesh.devices.reshape(Y, X, ZL, ZH, CORE), ("y", "x", "zl", "zh", "core"))
    rows, rep = ("y", "x", "zl"), ("zh", "core")
    in_specs = (P(rows + rep, None), P(rows + rep), P(rows, None), P(rows))
    out_specs = (P(rows, None), P(rows))
    return jax.shard_map(
        on_device, mesh=fine, in_specs=in_specs, out_specs=out_specs, check_vma=False
    )
```

time: 2150 us -> 90.6 us (0.04)
  blocking collectives: 1530 us -> 74.2 us
  waiting for transfers between devices: 584 us -> 1.56 us
    unnamed x2 -> x0, blocking collectives: 941 us -> none
    reduce_scatter x1 -> x0, waiting for transfers between devices: 584 us -> none  [on_device(): lax.psum_scatter(gram_term, 'rows', scatter_dimension=0, tiled=True)]
    all_gather x1, blocking collectives: 457 us -> 4.77 us  [on_device(): both = lax.all_gather(ring, 'core', axis=0, tiled=True)]
    psum x1 -> x0, blocking collectives: 134 us -> none  [on_device(): gram_out, moment_out = lax.psum((shares[0], shares[1]), 'rep')]
    all_to_all x0 -> x4, blocking collectives: none -> 69.4 us  [the longest x1 22.4 us: on_device(): run = lax.all_to_all(run, 'zl', 0, 0)]
where the time goes in v3:
time: 90.6 us; the launch traced here: 90.2 us
  blocking collectives  74.2 us (82%)
  starting transfers between devices  5.45 us (6%)
  Pallas kernels  5.24 us (6%)
  local copies, waits for them, and re-layouts  3.08 us (3%)
  waiting for transfers between devices  1.56 us (2%)
    all_to_all x1, blocking collectives, on_device(): run = lax.all_to_all(run, 'zl', 0, 0)  22.4 us
    all_to_all x1, blocking collectives, on_device(): ring = lax.all_to_all(ring, RING, 0, 0)  19.1 us
    all_to_all x1, blocking collectives, on_device(): plane = lax.all_to_all(plane, PLANE, 0, 0)  14.3 us
    all_to_all x1, blocking collectives, on_device(): terms = lax.all_to_all(terms, PLANE, 0, 0)  13.8 us
    ppermute x1, starting transfers between devices, on_device(): got = lax.ppermute(send, 'core', [(0, 1), (1, 0)])  5.45 us
    pallas_call x7, Pallas kernels, call(): pl.pallas_call(kernel, in_specs=[whole] * len(args), out_specs=(whole,) *...  5.24 us
    all_gather x1, blocking collectives, on_device(): both = lax.all_gather(ring, 'core', axis=0, tiled=True)  4.77 us
    unnamed x10, local copies, waits for them, and re-layouts  3.08 us
  transfers between devices with their start and end apart: 1, of which 1 were waited for; matrix products, arithmetic and copies ran while one was open for 0% of the time, Pallas kernels for 0%

profile of v3, /device:TPU:1, one launch (start us, length us, event | category | flops | bytes accessed | tf_op | source)
XLA Modules:
  0.0 90.2 jit_solution(8641121024335687649)
XLA Ops:
  0.6 0.0 copy-start
  0.6 0.6 copy-done
  1.3 0.0 copy-start.2
  1.3 0.7 copy-done.2
  2.0 0.1 pack_kernel.1
  2.1 22.4 %all_to_all.20.run_ref = bf16[8,16,128]{2,1,0:T(8,128)(2,1)S(1)} all-to-all(bf16[8,16,128]{2,1,0:T(8,128)(2,1)S(1)} %pack_kernel.1), channel_id=1, replica_groups=mesh['y'=4,'x'=4,'zl'=8,'zh'=2,'core'=2] {'zl'}, dimensions={0} | all-to-all | bytes 65536 | tf_op jit(solution)/shard_map/all_to_all | solution.py:207
  24.5 14.3 %all_to_all.21.plane_ref = bf16[16,72,128]{2,1,0:T(8,128)(2,1)S(1)} all-to-all(bf16[16,72,128]{2,1,0:T(8,128)(2,1)S(1)} %run_kernel.1), channel_id=1, replica_groups=mesh['y'=4,'x'=4,'zl'=8,'zh'=2,'core'=2] {'y','x'}, dimensions={0} | all-to-all | bytes 589824 | tf_op jit(solution)/shard_map/all_to_all | solution.py:209
  38.7 0.0 copy-start.3
  38.7 1.0 %copy-done.3 = bf16[2048,128]{1,0:T(8,128)(2,1)S(1)} copy-done((bf16[2048,128]{1,0:T(8,128)(2,1)S(1)}, bf16[2048,128]{1,0:T(8,128)(2,1)}, u32[]{:S(2)}) %copy-start.3) | copy-done | bytes 524312
  39.8 0.0 copy-start.4
  39.8 0.7 copy-done.4
  40.5 4.3 %gram_kernel.1 = (bf16[16,136,128]{2,1,0:T(8,128)(2,1)S(1)}, f32[16,136,128]{2,1,0:T(8,128)S(1)}) custom-call(bf16[2048,128]{1,0:T(8,128)(2,1)S(1)} %copy-done.3, s32[1,2048]{1,0:T(1,128)S(1)} %bitcast.5, bf16[16,72,128]{2,1,0:T(8,128)(2,1)S(1)} %all_to_all.21.plane_ref), custom_call_target="tpu_custom_call" | custom-call | flops 3221225472 | bytes 4194304 | tf_op jit(solution)/shard_map/gram_kernel/pallas_call | solution.py:26
  44.7 5.5 %collective-permute-start = (bf16[16,136,128]{2,1,0:T(8,128)(2,1)S(1)}, bf16[16,136,128]{2,1,0:T(8,128)(2,1)S(1)}, u32[]{:S(2)}, u32[]{:S(2)}) collective-permute-start(bf16[16,136,128]{2,1,0:T(8,128)(2,1)S(1)} %get-tuple-element.7), channel_id=1, source_target_pairs={{0,1},{1,0},{2,3},{3,2},{4,5},{5,4},{6,7},{7,6},{8,9},{9,8},{10,11... | collective-permute-start | bytes 1671176 | tf_op jit(solution)/shard_map/ppermute | solution.py:212
  50.2 1.6 %collective-permute-done.got_ref = bf16[16,136,128]{2,1,0:T(8,128)(2,1)S(1)} collective-permute-done((bf16[16,136,128]{2,1,0:T(8,128)(2,1)S(1)}, bf16[16,136,128]{2,1,0:T(8,128)(2,1)S(1)}, u32[]{:S(2)}, u32[]{:S(2)}) %collective-permute-start) | collective-permute-done | bytes 557088 | tf_op jit(solution)/shard_map/ppermute | solution.py:212
  51.8 0.1 pair_kernel.1
  51.9 0.0 copy-start.1
  51.9 13.8 %all_to_all.22.terms_ref = bf16[16,136,128]{2,1,0:T(8,128)(2,1)S(1)} all-to-all(bf16[16,136,128]{2,1,0:T(8,128)(2,1)S(1)} %pair_kernel.1), channel_id=1, replica_groups=mesh['y'=4,'x'=4,'zl'=8,'zh'=2,'core'=2] {'y','x'}, dimensions={0} | all-to-all | bytes 1114112 | tf_op jit(solution)/shard_map/all_to_all | solution.py:214
  65.7 0.1 plane_sum_kernel.1
  65.7 19.1 %all_to_all.23.terms_ref = bf16[16,24,128]{2,1,0:T(8,128)(2,1)S(1)} all-to-all(bf16[16,24,128]{2,1,0:T(8,128)(2,1)S(1)} %plane_sum_kernel.1), channel_id=1, replica_groups=mesh['y'=4,'x'=4,'zl'=8,'zh'=2,'core'=2] {'zh','zl'}, dimensions={0} | all-to-all | bytes 196608 | tf_op jit(solution)/shard_map/all_to_all | solution.py:217
  84.8 4.8 %all_gather.3.refs_0_ = f32[48,128]{1,0:T(8,128)S(1)} all-gather(f32[24,128]{1,0:T(8,128)S(1)} %ring_sum_kernel.1), channel_id=1, replica_groups=mesh['y'=4,'x'=4,'zl'=8,'zh'=2,'core'=2] {'core'}, dimensions={0}, use_global_device_ids=true | all-gather | bytes 36864 | tf_op jit(solution)/shard_map/all_gather | solution.py:219
  89.6 0.0 copy-done.1
  89.6 0.6 finish.1
  (2 shorter events, 0.1 us)
Async XLA Ops:
  0.6 0.7 copy-start
  1.3 0.7 copy-start.2
  38.7 1.0 %copy-start.3 = (bf16[2048,128]{1,0:T(8,128)(2,1)S(1)}, bf16[2048,128]{1,0:T(8,128)(2,1)}, u32[]{:S(2)}) copy-start(bf16[2048,128]{1,0:T(8,128)(2,1)} %rows_ref.1) | copy-start | bytes 1572868
  39.8 0.7 copy-start.4
  44.7 7.0 %collective-permute-start = (bf16[16,136,128]{2,1,0:T(8,128)(2,1)S(1)}, bf16[16,136,128]{2,1,0:T(8,128)(2,1)S(1)}, u32[]{:S(2)}, u32[]{:S(2)}) collective-permute-start(bf16[16,136,128]{2,1,0:T(8,128)(2,1)S(1)} %get-tuple-element.7), channel_id=1, source_target_pairs={{0,1},{1,0},{2,3},{3,2},{4,5},{5,4},{6,7},{7,6},{8,9},{9,8},{10,11... | collective-permute-start | bytes 1671176 | tf_op jit(solution)/shard_map/ppermute | solution.py:212
  51.9 37.7 %copy-start.1 = (bf16[8]{0:T(256)(128)(2,1)S(1)}, bf16[8]{0:T(256)(128)(2,1)}, u32[]{:S(2)}) copy-start(bf16[8]{0:T(256)(128)(2,1)} %param.7) | copy-start | bytes 52

commit v4 on v3

--- a/solution.py
+++ b/solution.py
@@ -12,7 +12,8 @@
 OWN = 8
 RUN = ZL * OWN
 MASKS = 16
-BLOCK = 1024
+BLOCK = 2048
+FIRST = 4
 GROUP = 16
 LANES = 128
 NT = (((1,), (1,)), ((), ()))
@@ -20,12 +21,17 @@
 gamma_rate = 0.03125
 
 
-def call(kernel, out_shape, *args, scratch=(), cost=None, vmem=16 << 20):
+def run_groups():
+    near = [FIRST + (low - FIRST) % ZL for low in range(ZL)]
+    return [near, [(place + ZL) % (ZH * ZL) for place in near]]
+
+
+def call(kernel, out_shape, *args, scratch=(), cost=None, vmem=16 << 20, space=pltpu.VMEM):
     whole = pl.BlockSpec(memory_space=pltpu.VMEM)
     several = isinstance(out_shape, tuple)
     return pl.pallas_call(
         kernel,
-        in_specs=[whole] * len(args),
+        in_specs=[pl.BlockSpec(memory_space=space)] * len(args),
         out_specs=(whole,) * len(out_shape) if several else whole,
         out_shape=out_shape,
         scratch_shapes=list(scratch),
@@ -204,8 +210,13 @@
     bf16, f32 = jnp.bfloat16, jnp.float32
     treat_row = land_treat.reshape(1, OWN)
     run = call(pack_kernel, jax.ShapeDtypeStruct((ZL, 2 * OWN, width), bf16), landmarks, treat_row)
-    run = lax.all_to_all(run, "zl", 0, 0)
-    plane = call(run_kernel, jax.ShapeDtypeStruct((Y * X, RUN + 8, width), bf16), run)
+    run = lax.all_to_all(run, RING, 0, 0, axis_index_groups=run_groups())
+    plane = call(
+        run_kernel,
+        jax.ShapeDtypeStruct((Y * X, RUN + 8, width), bf16),
+        run,
+        cost=pl.CostEstimate(flops=1 << 32, transcendentals=0, bytes_accessed=1 << 25),
+    )
     plane = lax.all_to_all(plane, PLANE, 0, 0)
 
     send, keep = chip_gram(covariates, treated.reshape(1, count), plane)

time: 90.6 us -> 84.2 us (0.929)
  blocking collectives: 74.2 us -> 69.9 us
  local copies, waits for them, and re-layouts: 3.08 us -> 1.35 us
    all_to_all x1, blocking collectives: 22.4 us -> 19.3 us  [on_device(): run = lax.all_to_all(run, RING, 0, 0, axis_index_groups=run_groups())]
    unnamed x10, local copies, waits for them, and re-layouts: 3.08 us -> 1.35 us
    all_to_all x1, blocking collectives: 19.1 us -> 17.7 us  [on_device(): ring = lax.all_to_all(ring, RING, 0, 0)]
where the time goes in v4:
time: 84.2 us; the launch traced here: 83.9 us
  blocking collectives  69.9 us (83%)
  starting transfers between devices  5.44 us (6%)
  Pallas kernels  5.02 us (6%)
  waiting for transfers between devices  1.56 us (2%)
  local copies, waits for them, and re-layouts  1.35 us (2%)
    all_to_all x1, blocking collectives, on_device(): run = lax.all_to_all(run, RING, 0, 0, axis_index_groups=run_groups())  19.3 us
    all_to_all x1, blocking collectives, on_device(): ring = lax.all_to_all(ring, RING, 0, 0)  17.7 us
    all_to_all x1, blocking collectives, on_device(): plane = lax.all_to_all(plane, PLANE, 0, 0)  14.4 us
    all_to_all x1, blocking collectives, on_device(): terms = lax.all_to_all(terms, PLANE, 0, 0)  13.8 us
    ppermute x1, starting transfers between devices, on_device(): got = lax.ppermute(send, 'core', [(0, 1), (1, 0)])  5.44 us
    pallas_call x7, Pallas kernels, call(): pl.pallas_call(kernel, in_specs=[pl.BlockSpec(memory_space=space)] * len(...  5.02 us
    all_gather x1, blocking collectives, on_device(): both = lax.all_gather(ring, 'core', axis=0, tiled=True)  4.77 us
  transfers between devices with their start and end apart: 1, of which 1 were waited for; matrix products, arithmetic and copies ran while one was open for 0% of the time, Pallas kernels for 0%

profile of v4, /device:TPU:1, one launch (start us, length us, event | category | flops | bytes accessed | tf_op | source)
XLA Modules:
  0.0 83.9 jit_solution(5709492734813533524)
XLA Ops:
  0.6 0.0 copy-start
  0.6 0.6 copy-done
  1.3 0.0 copy-start.2
  1.3 0.7 copy-done.2
  2.0 0.1 pack_kernel.1
  2.1 19.3 %all_to_all.20.run_ref = bf16[8,16,128]{2,1,0:T(8,128)(2,1)S(1)} all-to-all(bf16[8,16,128]{2,1,0:T(8,128)(2,1)S(1)} %pack_kernel.1), channel_id=1, replica_groups={{2,6,10,14,16,20,24,28},{0,4,8,12,18,22,26,30},{3,7,11,15,17,21,25,29},..., dimensions={0} | all-to-all | bytes 65536 | tf_op jit(solution)/shard_map/all_to_all | solution.py:213
  21.3 0.0 copy-start.3
  21.3 0.0 copy-start.4
  21.4 14.4 %all_to_all.21.plane_ref = bf16[16,72,128]{2,1,0:T(8,128)(2,1)S(1)} all-to-all(bf16[16,72,128]{2,1,0:T(8,128)(2,1)S(1)} %run_kernel.1), channel_id=1, replica_groups=mesh['y'=4,'x'=4,'zl'=8,'zh'=2,'core'=2] {'y','x'}, dimensions={0} | all-to-all | bytes 589824 | tf_op jit(solution)/shard_map/all_to_all | solution.py:220
  35.8 0.0 copy-done.3
  35.8 0.0 copy-done.4
  35.8 4.0 %gram_kernel.1 = (bf16[16,136,128]{2,1,0:T(8,128)(2,1)S(1)}, f32[16,136,128]{2,1,0:T(8,128)S(1)}) custom-call(bf16[2048,128]{1,0:T(8,128)(2,1)S(1)} %copy-done.3, s32[1,2048]{1,0:T(1,128)S(1)} %bitcast.5, bf16[16,72,128]{2,1,0:T(8,128)(2,1)S(1)} %all_to_all.21.plane_ref), custom_call_target="tpu_custom_call" | custom-call | flops 3221225472 | bytes 4194304 | tf_op jit(solution)/shard_map/gram_kernel/pallas_call | solution.py:32
  39.8 5.4 %collective-permute-start = (bf16[16,136,128]{2,1,0:T(8,128)(2,1)S(1)}, bf16[16,136,128]{2,1,0:T(8,128)(2,1)S(1)}, u32[]{:S(2)}, u32[]{:S(2)}) collective-permute-start(bf16[16,136,128]{2,1,0:T(8,128)(2,1)S(1)} %get-tuple-element.7), channel_id=1, source_target_pairs={{0,1},{1,0},{2,3},{3,2},{4,5},{5,4},{6,7},{7,6},{8,9},{9,8},{10,11... | collective-permute-start | bytes 1671176 | tf_op jit(solution)/shard_map/ppermute | solution.py:223
  45.3 1.6 %collective-permute-done.got_ref = bf16[16,136,128]{2,1,0:T(8,128)(2,1)S(1)} collective-permute-done((bf16[16,136,128]{2,1,0:T(8,128)(2,1)S(1)}, bf16[16,136,128]{2,1,0:T(8,128)(2,1)S(1)}, u32[]{:S(2)}, u32[]{:S(2)}) %collective-permute-start) | collective-permute-done | bytes 557088 | tf_op jit(solution)/shard_map/ppermute | solution.py:223
  46.9 0.1 pair_kernel.1
  47.0 0.0 copy-start.1
  47.0 13.8 %all_to_all.22.terms_ref = bf16[16,136,128]{2,1,0:T(8,128)(2,1)S(1)} all-to-all(bf16[16,136,128]{2,1,0:T(8,128)(2,1)S(1)} %pair_kernel.1), channel_id=1, replica_groups=mesh['y'=4,'x'=4,'zl'=8,'zh'=2,'core'=2] {'y','x'}, dimensions={0} | all-to-all | bytes 1114112 | tf_op jit(solution)/shard_map/all_to_all | solution.py:225
  60.8 0.1 plane_sum_kernel.1
  60.8 17.7 %all_to_all.23.terms_ref = bf16[16,24,128]{2,1,0:T(8,128)(2,1)S(1)} all-to-all(bf16[16,24,128]{2,1,0:T(8,128)(2,1)S(1)} %plane_sum_kernel.1), channel_id=1, replica_groups=mesh['y'=4,'x'=4,'zl'=8,'zh'=2,'core'=2] {'zh','zl'}, dimensions={0} | all-to-all | bytes 196608 | tf_op jit(solution)/shard_map/all_to_all | solution.py:228
  78.5 4.8 %all_gather.3.refs_0_ = f32[48,128]{1,0:T(8,128)S(1)} all-gather(f32[24,128]{1,0:T(8,128)S(1)} %ring_sum_kernel.1), channel_id=1, replica_groups=mesh['y'=4,'x'=4,'zl'=8,'zh'=2,'core'=2] {'core'}, dimensions={0}, use_global_device_ids=true | all-gather | bytes 36864 | tf_op jit(solution)/shard_map/all_gather | solution.py:230
  83.3 0.0 copy-done.1
  83.3 0.6 finish.1
  (2 shorter events, 0.1 us)
Async XLA Ops:
  0.6 0.7 copy-start
  1.3 0.7 copy-start.2
  21.3 14.5 %copy-start.3 = (bf16[2048,128]{1,0:T(8,128)(2,1)S(1)}, bf16[2048,128]{1,0:T(8,128)(2,1)}, u32[]{:S(2)}) copy-start(bf16[2048,128]{1,0:T(8,128)(2,1)} %rows_ref.1) | copy-start | bytes 1572868
  21.3 14.5 %copy-start.4 = (s32[2048]{0:T(1024)S(1)}, s32[2048]{0:T(1024)}, u32[]{:S(2)}) copy-start(s32[2048]{0:T(1024)} %param.5) | copy-start | bytes 24580
  39.8 7.0 %collective-permute-start = (bf16[16,136,128]{2,1,0:T(8,128)(2,1)S(1)}, bf16[16,136,128]{2,1,0:T(8,128)(2,1)S(1)}, u32[]{:S(2)}, u32[]{:S(2)}) collective-permute-start(bf16[16,136,128]{2,1,0:T(8,128)(2,1)S(1)} %get-tuple-element.7), channel_id=1, source_target_pairs={{0,1},{1,0},{2,3},{3,2},{4,5},{5,4},{6,7},{7,6},{8,9},{9,8},{10,11... | collective-permute-start | bytes 1671176 | tf_op jit(solution)/shard_map/ppermute | solution.py:223
  47.0 36.3 %copy-start.1 = (bf16[8]{0:T(256)(128)(2,1)S(1)}, bf16[8]{0:T(256)(128)(2,1)}, u32[]{:S(2)}) copy-start(bf16[8]{0:T(256)(128)(2,1)} %param.7) | copy-start | bytes 52

commit v5 on v4

--- a/solution.py
+++ b/solution.py
@@ -51,7 +51,12 @@
     return high, middle, value - high - middle
 
 
-def pack_kernel(land_ref, treat_ref, out_ref):
+def ones_kernel(out_ref):
+    lane = lax.broadcasted_iota(jnp.int32, (OWN, LANES), 1) - GROUP * lax.axis_index("zl")
+    out_ref[...] = jnp.where((lane >= 0) & (lane < 3), 1.0, 0.0)
+
+
+def pack_kernel(land_ref, treat_ref, ones_ref, out_ref):
     land = land_ref[...].astype(jnp.float32)
     row = lax.broadcasted_iota(jnp.int32, (OWN, OWN), 0)
     col = lax.broadcasted_iota(jnp.int32, (OWN, OWN), 1)
@@ -59,7 +64,7 @@
     treat = jnp.sum(jnp.where(row == col, treat, 0.0), axis=1, keepdims=True)
     own = -gamma_rate * jnp.sum(land * land, axis=1, keepdims=True) - 0.5 * treat * treat
     lane = lax.broadcasted_iota(jnp.int32, (OWN, LANES), 1) - GROUP * lax.axis_index("zl")
-    extra = jnp.where((lane >= 0) & (lane < 3), 1.0, 0.0)
+    extra = ones_ref[...]
     for at, part in enumerate((treat,) + three_parts(own)):
         extra = jnp.where(lane == 3 + at, part, extra)
     land = (land * (2.0 * gamma_rate)).astype(jnp.bfloat16)
@@ -80,8 +85,50 @@
         out_ref[place, RUN:] = extra
 
 
-def gram_kernel(rows_ref, flag_ref, plane_ref, send_ref, keep_ref, land, feat, acc):
-    core = lax.axis_index("core")
+def hide_sums(parity):
+    row = lax.broadcasted_iota(jnp.int32, (RUN, LANES), 0)
+    lane = lax.broadcasted_iota(jnp.int32, (RUN, LANES), 1)
+    block = row // OWN == (lane - RUN * parity) // OWN
+    block = block & (lane >= RUN * parity)
+    at, col = row % OWN, lane % OWN
+    return (
+        block & (at == 7) & (col < 7),
+        block & (at == 6) & (col < 6),
+        block & (at == 5) & (col < 3),
+    )
+
+
+def half_gram(which, feat, out_ref, acc):
+    per_panel = Y * X // PANELS
+    size = per_panel * RUN
+    half = size // CORE
+    masks = [hide_sums(parity) for parity in range(LANES // RUN)]
+    first_col = lax.broadcasted_iota(jnp.int32, (1, LANES), 1) % OWN == 0
+    for panel in range(PANELS):
+        mine = feat[panel, pl.ds(pl.multiple_of(which * half, half), half), :]
+        acc[...] = lax.dot_general(feat[panel], mine, NT, preferred_element_type=jnp.float32)
+        for spot in range(per_panel):
+            place, first = panel * per_panel + spot, spot * RUN
+            for tile in range(half // LANES):
+                lanes = slice(tile * LANES, (tile + 1) * LANES)
+                value = acc[first : first + RUN, lanes]
+                if tile == (first % half) // LANES:
+                    sums = acc[size : size + 8, lanes]
+                    tail = jnp.where(
+                        first_col,
+                        pltpu.roll(sums, LANES - 7, 1)[0:1],
+                        pltpu.roll(sums, LANES - 5, 1)[1:2],
+                    )
+                    hidden = value
+                    for mask, part in zip(
+                        masks[spot % (LANES // RUN)], (sums[0:1], sums[1:2], tail), strict=True
+                    ):
+                        hidden = jnp.where(mask, part, hidden)
+                    value = jnp.where(which == first // half, hidden, value)
+                out_ref[place, tile * RUN : (tile + 1) * RUN, :] = value.astype(out_ref.dtype)
+
+
+def send_kernel(rows_ref, flag_ref, plane_ref, send_ref, feat, land, acc):
     per_panel = Y * X // PANELS
     size = per_panel * RUN
     half = size // CORE
@@ -120,45 +167,47 @@
             arg = lax.dot_general(land[panel], wide, NT, preferred_element_type=jnp.float32)
             feat[panel, :size, at : at + BLOCK] = jnp.exp(arg).astype(jnp.bfloat16)
             feat[panel, size:, at : at + BLOCK] = mask.astype(jnp.bfloat16)
-    for panel in range(PANELS):
-        for which, out_ref in ((1 - core, send_ref), (core, keep_ref)):
-            mine = feat[panel, pl.ds(pl.multiple_of(which * half, half), half), :]
-            acc[...] = lax.dot_general(feat[panel], mine, NT, preferred_element_type=jnp.float32)
-            for spot in range(per_panel):
-                place, first = panel * per_panel + spot, spot * RUN
-                for tile in range(half // LANES):
-                    out_ref[place, tile * RUN : (tile + 1) * RUN, :] = acc[
-                        first : first + RUN, tile * LANES : (tile + 1) * LANES
-                    ].astype(out_ref.dtype)
-                lanes = (first % half) // LANES * LANES
-                sums = acc[size : size + 8, lanes : lanes + LANES]
-                sums = jnp.where(which == first // half, sums, 0.0)
-                out_ref[place, half // LANES * RUN :, :] = sums.astype(out_ref.dtype)
+    half_gram(1 - lax.axis_index("core"), feat, send_ref, acc)
+
+
+def keep_kernel(feat, keep_ref, acc):
+    half_gram(lax.axis_index("core"), feat, keep_ref, acc)
 
 
 def chip_gram(rows, flag, plane):
     size = Y * X // PANELS * RUN
     half = size // CORE
-    shape = (Y * X, half // LANES * RUN + 8, LANES)
+    shape = (Y * X, half // LANES * RUN, LANES)
     count, width = rows.shape
-    return call(
-        gram_kernel,
-        (jax.ShapeDtypeStruct(shape, jnp.bfloat16), jax.ShapeDtypeStruct(shape, jnp.float32)),
+    acc = pltpu.VMEM((size + MASKS, half), jnp.float32)
+    flops = 2 * count * PANELS * size * half
+    send, feat = call(
+        send_kernel,
+        (
+            jax.ShapeDtypeStruct(shape, jnp.bfloat16),
+            jax.ShapeDtypeStruct((PANELS, size + MASKS, count), jnp.bfloat16),
+        ),
         rows,
         flag,
         plane,
-        scratch=[
-            pltpu.VMEM((PANELS, size, 2 * LANES), jnp.bfloat16),
-            pltpu.VMEM((PANELS, size + MASKS, count), jnp.bfloat16),
-            pltpu.VMEM((size + MASKS, half), jnp.float32),
-        ],
+        scratch=[pltpu.VMEM((PANELS, size, 2 * LANES), jnp.bfloat16), acc],
         cost=pl.CostEstimate(
-            flops=2 * count * PANELS * size * (size + 2 * width),
+            flops=flops + 4 * count * PANELS * size * width,
             transcendentals=count * PANELS * size,
-            bytes_accessed=4 << 20,
+            bytes_accessed=6 << 20,
         ),
-        vmem=40 << 20,
-    )
+        vmem=32 << 20,
+    )
+    got = lax.ppermute(send, "core", [(0, 1), (1, 0)])
+    keep = call(
+        keep_kernel,
+        jax.ShapeDtypeStruct(shape, jnp.float32),
+        feat,
+        scratch=[acc],
+        cost=pl.CostEstimate(flops=flops, transcendentals=0, bytes_accessed=6 << 20),
+        vmem=16 << 20,
+    )
+    return got, keep
 
 
 def pair_kernel(keep_ref, got_ref, out_ref):
@@ -170,13 +219,12 @@
     for place in range(1, Y * X):
         total += terms_ref[place].astype(jnp.float32)
     total = total.astype(jnp.bfloat16)
-    tiles = (total.shape[0] - 8) // RUN
+    tiles = total.shape[0] // RUN
     for high in range(ZH):
         for low in range(ZL):
             for tile in range(tiles):
                 at = tile * RUN + low * OWN
                 out_ref[high * ZL + low, tile * OWN : (tile + 1) * OWN] = total[at : at + OWN]
-            out_ref[high * ZL + low, tiles * OWN :] = total[tiles * RUN :]
 
 
 def ring_sum_kernel(terms_ref, out_ref):
@@ -187,20 +235,28 @@
 
 
 def finish_kernel(scale, both_ref, treat_ref, gram_ref, moment_ref):
-    rows = both_ref.shape[0] // CORE
-    tiles = (rows - 8) // OWN
-    for core in range(CORE):
-        for tile in range(tiles):
-            at = core * tiles + tile
-            first = core * rows + tile * OWN
-            gram_ref[:, at * LANES : (at + 1) * LANES] = both_ref[first : first + OWN] * scale
-    sums = both_ref[tiles * OWN : rows] + both_ref[rows + tiles * OWN :]
-    at = RUN * (lax.axis_index("x") % (LANES // RUN)) + OWN * lax.axis_index("zl")
-    sums = pltpu.roll(sums, (LANES - at) % LANES, 1)
+    tiles = both_ref.shape[0] // OWN
+    for at in range(tiles):
+        gram_ref[:, at * LANES : (at + 1) * LANES] = both_ref[at * OWN : (at + 1) * OWN] * scale
+    y, x = lax.axis_index("y"), lax.axis_index("x")
+    per_row = LANES // RUN
+    spot = (y % (Y // PANELS)) * X + x
+    at = spot // per_row
+    shift = RUN * (spot % per_row) + OWN * lax.axis_index("zl")
+    block = both_ref[pl.ds(pl.multiple_of(at * OWN, OWN), OWN), :]
+    block = pltpu.roll(block, (LANES - shift) % LANES, 1)
+    row = lax.broadcasted_iota(jnp.int32, (OWN, LANES), 0)
+    lane = lax.broadcasted_iota(jnp.int32, (OWN, LANES), 1)
+    mirror = jnp.concatenate([block, jnp.zeros((LANES - OWN, LANES), jnp.float32)], axis=0).T[:OWN]
+    whole = pltpu.roll(jnp.where(lane < row, mirror, block), shift, 1)
+    gram_ref[:, pl.ds(pl.multiple_of(at * LANES, LANES), LANES)] = whole * scale
+    lane = lane[:1]
+    sum_one = jnp.where(lane < 7, block[7:8], pltpu.roll(block, 7, 1)[5:6])
+    sum_zero = jnp.where(lane < 6, block[6:7], pltpu.roll(block, 5, 1)[5:6])
     treat = treat_ref[...].astype(jnp.float32)
     on_one = jnp.exp(-0.5 * jnp.square(1.0 - treat))
     on_zero = jnp.exp(-0.5 * jnp.square(treat))
-    kern = sums[0:1, :OWN] / on_one + sums[1:2, :OWN] / on_zero
+    kern = sum_one[:, :OWN] / on_one + sum_zero[:, :OWN] / on_zero
     moment_ref[...] = (on_one - on_zero) * (kern * scale)
 
 
@@ -209,21 +265,23 @@
     scale = 1.0 / (count * Y * X * ZL * ZH * CORE)
     bf16, f32 = jnp.bfloat16, jnp.float32
     treat_row = land_treat.reshape(1, OWN)
-    run = call(pack_kernel, jax.ShapeDtypeStruct((ZL, 2 * OWN, width), bf16), landmarks, treat_row)
+    early = pl.CostEstimate(flops=1 << 32, transcendentals=0, bytes_accessed=1 << 25)
+    ones = call(ones_kernel, jax.ShapeDtypeStruct((OWN, LANES), f32), cost=early)
+    packed = jax.ShapeDtypeStruct((ZL, 2 * OWN, width), bf16)
+    run = call(pack_kernel, packed, landmarks, treat_row, ones)
     run = lax.all_to_all(run, RING, 0, 0, axis_index_groups=run_groups())
     plane = call(
         run_kernel,
         jax.ShapeDtypeStruct((Y * X, RUN + 8, width), bf16),
         run,
-        cost=pl.CostEstimate(flops=1 << 32, transcendentals=0, bytes_accessed=1 << 25),
+        cost=early,
     )
     plane = lax.all_to_all(plane, PLANE, 0, 0)
 
-    send, keep = chip_gram(covariates, treated.reshape(1, count), plane)
-    got = lax.ppermute(send, "core", [(0, 1), (1, 0)])
-    terms = call(pair_kernel, jax.ShapeDtypeStruct(send.shape, bf16), keep, got)
+    got, keep = chip_gram(covariates, treated.reshape(1, count), plane)
+    terms = call(pair_kernel, jax.ShapeDtypeStruct(got.shape, bf16), keep, got)
     terms = lax.all_to_all(terms, PLANE, 0, 0)
-    rows = (terms.shape[1] - 8) // ZL + 8
+    rows = terms.shape[1] // ZL
     ring = call(plane_sum_kernel, jax.ShapeDtypeStruct((ZH * ZL, rows, LANES), bf16), terms)
     ring = lax.all_to_all(ring, RING, 0, 0)
     ring = call(ring_sum_kernel, jax.ShapeDtypeStruct((rows, LANES), f32), ring)
@@ -235,7 +293,7 @@
     gram, moment = call(
         finish,
         (
-            jax.ShapeDtypeStruct((OWN, CORE * (rows - 8) // OWN * LANES), f32),
+            jax.ShapeDtypeStruct((OWN, CORE * rows // OWN * LANES), f32),
             jax.ShapeDtypeStruct((1, OWN), f32),
         ),
         both,

time: 84.2 us -> 82.1 us (0.975)
  waiting for transfers between devices: 1.56 us -> 0.03 us
    ppermute x1, waiting for transfers between devices: 1.56 us -> 0.03 us  [chip_gram(): got = lax.ppermute(send, 'core', [(0, 1), (1, 0)])]
    pallas_call x7 -> x9, Pallas kernels: 5.02 us -> 5.79 us  [call(): pl.pallas_call(kernel, in_specs=[pl.BlockSpec(memory_space=space)] * len(...]
  transfers between devices with their start and end apart: 1 -> 1, of which waited for: 1 -> 0; matrix products, arithmetic and copies ran while one was open for 0% -> 0% of each run, Pallas kernels for 0% -> 2%
where the time goes in v5:
time: 82.1 us; the launch traced here: 81.8 us
  blocking collectives  69.2 us (84%)
  Pallas kernels  5.79 us (7%)
  starting transfers between devices  5.44 us (7%)
    all_to_all x1, blocking collectives, on_device(): run = lax.all_to_all(run, RING, 0, 0, axis_index_groups=run_groups())  19.3 us
    all_to_all x1, blocking collectives, on_device(): ring = lax.all_to_all(ring, RING, 0, 0)  17.4 us
    all_to_all x1, blocking collectives, on_device(): plane = lax.all_to_all(plane, PLANE, 0, 0)  14.4 us
    all_to_all x1, blocking collectives, on_device(): terms = lax.all_to_all(terms, PLANE, 0, 0)  13.4 us
    pallas_call x9, Pallas kernels, call(): pl.pallas_call(kernel, in_specs=[pl.BlockSpec(memory_space=space)] * len(...  5.79 us
    ppermute x1, starting transfers between devices, chip_gram(): got = lax.ppermute(send, 'core', [(0, 1), (1, 0)])  5.44 us
    all_gather x1, blocking collectives, on_device(): both = lax.all_gather(ring, 'core', axis=0, tiled=True)  4.75 us
  transfers between devices with their start and end apart: 1, of which 0 were waited for; matrix products, arithmetic and copies ran while one was open for 0% of the time, Pallas kernels for 2%

profile of v5, /device:TPU:1, one launch (start us, length us, event | category | flops | bytes accessed | tf_op | source)
XLA Modules:
  0.0 81.8 jit_solution(11010572545049339872)
XLA Ops:
  0.6 0.0 copy-start
  0.6 0.0 copy-start.1
  0.7 0.6 copy-done
  1.3 0.0 copy-done.1
  1.3 0.1 pack_kernel.1
  1.4 19.3 %all_to_all.20.run_ref = bf16[8,16,128]{2,1,0:T(8,128)(2,1)S(1)} all-to-all(bf16[8,16,128]{2,1,0:T(8,128)(2,1)S(1)} %pack_kernel.1), channel_id=1, replica_groups={{2,6,10,14,16,20,24,28},{0,4,8,12,18,22,26,30},{3,7,11,15,17,21,25,29},..., dimensions={0} | all-to-all | bytes 65536 | tf_op jit(solution)/shard_map/all_to_all | solution.py:272
  20.7 0.0 copy-start.2
  20.7 0.0 copy-start.3
  20.7 14.4 %all_to_all.21.plane_ref = bf16[16,72,128]{2,1,0:T(8,128)(2,1)S(1)} all-to-all(bf16[16,72,128]{2,1,0:T(8,128)(2,1)S(1)} %run_kernel.1), channel_id=1, replica_groups=mesh['y'=4,'x'=4,'zl'=8,'zh'=2,'core'=2] {'y','x'}, dimensions={0} | all-to-all | bytes 589824 | tf_op jit(solution)/shard_map/all_to_all | solution.py:279
  35.1 0.0 copy-done.2
  35.2 0.0 copy-done.3
  35.2 3.2 %send_kernel.1 = (bf16[16,128,128]{2,1,0:T(8,128)(2,1)S(1)}, bf16[2,528,2048]{2,1,0:T(8,128)(2,1)S(1)}) custom-call(bf16[2048,128]{1,0:T(8,128)(2,1)S(1)} %copy-done.2, s32[1,2048]{1,0:T(1,128)S(1)} %bitcast.5, bf16[16,72,128]{2,1,0:T(8,128)(2,1)S(1)} %all_to_all.21.plane_ref), custom_call_target="tpu_custom_call" | custom-call | flops 2147483648 | bytes 6291456 | tf_op jit(solution)/shard_map/send_kernel/pallas_call | solution.py:32
  38.3 5.4 %collective-permute-start = (bf16[16,128,128]{2,1,0:T(8,128)(2,1)S(1)}, bf16[16,128,128]{2,1,0:T(8,128)(2,1)S(1)}, u32[]{:S(2)}, u32[]{:S(2)}) collective-permute-start(bf16[16,128,128]{2,1,0:T(8,128)(2,1)S(1)} %get-tuple-element.7), channel_id=1, source_target_pairs={{0,1},{1,0},{2,3},{3,2},{4,5},{5,4},{6,7},{7,6},{8,9},{9,8},{10,11... | collective-permute-start | bytes 1572872 | tf_op jit(solution)/shard_map/ppermute | solution.py:201
  43.8 1.5 %keep_kernel.1.keep_ref = f32[16,128,128]{2,1,0:T(8,128)S(1)} custom-call(bf16[2,528,2048]{2,1,0:T(8,128)(2,1)S(1)} %get-tuple-element.6.feat), custom_call_target="tpu_custom_call" | custom-call | flops 1073741824 | bytes 6291456 | tf_op jit(solution)/shard_map/keep_kernel/pallas_call | solution.py:32
  45.2 0.0 collective-permute-done.got_ref
  45.3 0.1 pair_kernel.1
  45.4 13.4 %all_to_all.22.terms_ref = bf16[16,128,128]{2,1,0:T(8,128)(2,1)S(1)} all-to-all(bf16[16,128,128]{2,1,0:T(8,128)(2,1)S(1)} %pair_kernel.1), channel_id=1, replica_groups=mesh['y'=4,'x'=4,'zl'=8,'zh'=2,'core'=2] {'y','x'}, dimensions={0} | all-to-all | bytes 1048576 | tf_op jit(solution)/shard_map/all_to_all | solution.py:283
  58.7 0.1 plane_sum_kernel.1
  58.8 17.4 %all_to_all.23.terms_ref = bf16[16,16,128]{2,1,0:T(8,128)(2,1)S(1)} all-to-all(bf16[16,16,128]{2,1,0:T(8,128)(2,1)S(1)} %plane_sum_kernel.1), channel_id=1, replica_groups=mesh['y'=4,'x'=4,'zl'=8,'zh'=2,'core'=2] {'zh','zl'}, dimensions={0} | all-to-all | bytes 131072 | tf_op jit(solution)/shard_map/all_to_all | solution.py:286
  76.2 4.8 %all_gather.3.refs_0_ = f32[32,128]{1,0:T(8,128)S(1)} all-gather(f32[16,128]{1,0:T(8,128)S(1)} %ring_sum_kernel.1), channel_id=1, replica_groups=mesh['y'=4,'x'=4,'zl'=8,'zh'=2,'core'=2] {'core'}, dimensions={0}, use_global_device_ids=true | all-gather | bytes 24576 | tf_op jit(solution)/shard_map/all_gather | solution.py:288
  81.0 0.8 %finish.1 = (f32[8,512]{1,0:T(8,128)}, f32[1,8]{1,0:T(1,128)}) custom-call(f32[32,128]{1,0:T(8,128)S(1)} %all_gather.3.refs_0_, bf16[1,8]{1,0:T(2,128)(2,1)S(1)} %bitcast.4), custom_call_target="tpu_custom_call" | custom-call | tf_op jit(solution)/shard_map/finish/pallas_call | solution.py:32
  (3 shorter events, 0.1 us)
Async XLA Ops:
  0.6 0.7 copy-start
  0.6 0.7 copy-start.1
  20.7 14.5 %copy-start.2 = (bf16[2048,128]{1,0:T(8,128)(2,1)S(1)}, bf16[2048,128]{1,0:T(8,128)(2,1)}, u32[]{:S(2)}) copy-start(bf16[2048,128]{1,0:T(8,128)(2,1)} %rows_ref.1) | copy-start | bytes 1572868
  20.7 14.5 %copy-start.3 = (s32[2048]{0:T(1024)S(1)}, s32[2048]{0:T(1024)}, u32[]{:S(2)}) copy-start(s32[2048]{0:T(1024)} %param.5) | copy-start | bytes 24580
  38.3 7.0 %collective-permute-start = (bf16[16,128,128]{2,1,0:T(8,128)(2,1)S(1)}, bf16[16,128,128]{2,1,0:T(8,128)(2,1)S(1)}, u32[]{:S(2)}, u32[]{:S(2)}) collective-permute-start(bf16[16,128,128]{2,1,0:T(8,128)(2,1)S(1)} %get-tuple-element.7), channel_id=1, source_target_pairs={{0,1},{1,0},{2,3},{3,2},{4,5},{5,4},{6,7},{7,6},{8,9},{9,8},{10,11... | collective-permute-start | bytes 1572872 | tf_op jit(solution)/shard_map/ppermute | solution.py:201

commit v6 on v5

--- a/solution.py
+++ b/solution.py
@@ -14,6 +14,10 @@
 MASKS = 16
 BLOCK = 2048
 FIRST = 4
+NEAR_LEAD, RING_LEAD, PLANE_LEAD = 0, 10, 10
+NEAR_ORDER = [(NEAR_LEAD + step) % ZL for step in range(ZL)]
+RING_ORDER = [(RING_LEAD + step) % (ZH * ZL) for step in range(ZH * ZL)]
+PLANE_ORDER = [(PLANE_LEAD + step) % (Y * X) for step in range(Y * X)]
 GROUP = 16
 LANES = 128
 NT = (((1,), (1,)), ((), ()))
@@ -22,7 +26,7 @@
 
 
 def run_groups():
-    near = [FIRST + (low - FIRST) % ZL for low in range(ZL)]
+    near = [FIRST + (low - FIRST) % ZL for low in NEAR_ORDER]
     return [near, [(place + ZL) % (ZH * ZL) for place in near]]
 
 
@@ -81,7 +85,7 @@
     extra = extra.astype(jnp.bfloat16)
     for place in range(Y * X):
         for part in range(ZL):
-            out_ref[place, part * OWN : (part + 1) * OWN] = run_ref[part, :OWN]
+            out_ref[place, part * OWN : (part + 1) * OWN] = run_ref[NEAR_ORDER.index(part), :OWN]
         out_ref[place, RUN:] = extra
 
 
@@ -98,46 +102,46 @@
     )
 
 
-def half_gram(which, feat, out_ref, acc):
+def half_gram(which, panel, feat, out_ref):
     per_panel = Y * X // PANELS
     size = per_panel * RUN
     half = size // CORE
     masks = [hide_sums(parity) for parity in range(LANES // RUN)]
     first_col = lax.broadcasted_iota(jnp.int32, (1, LANES), 1) % OWN == 0
-    for panel in range(PANELS):
-        mine = feat[panel, pl.ds(pl.multiple_of(which * half, half), half), :]
-        acc[...] = lax.dot_general(feat[panel], mine, NT, preferred_element_type=jnp.float32)
-        for spot in range(per_panel):
-            place, first = panel * per_panel + spot, spot * RUN
-            for tile in range(half // LANES):
-                lanes = slice(tile * LANES, (tile + 1) * LANES)
-                value = acc[first : first + RUN, lanes]
-                if tile == (first % half) // LANES:
-                    sums = acc[size : size + 8, lanes]
-                    tail = jnp.where(
-                        first_col,
-                        pltpu.roll(sums, LANES - 7, 1)[0:1],
-                        pltpu.roll(sums, LANES - 5, 1)[1:2],
-                    )
-                    hidden = value
-                    for mask, part in zip(
-                        masks[spot % (LANES // RUN)], (sums[0:1], sums[1:2], tail), strict=True
-                    ):
-                        hidden = jnp.where(mask, part, hidden)
-                    value = jnp.where(which == first // half, hidden, value)
-                out_ref[place, tile * RUN : (tile + 1) * RUN, :] = value.astype(out_ref.dtype)
-
-
-def send_kernel(rows_ref, flag_ref, plane_ref, send_ref, feat, land, acc):
+    mine = feat[pl.ds(pl.multiple_of(which * half, half), half), :]
+    gram = lax.dot_general(feat[...], mine, NT, preferred_element_type=jnp.float32)
+    for spot in range(per_panel):
+        place, first = PLANE_ORDER.index(panel * per_panel + spot), spot * RUN
+        for tile in range(half // LANES):
+            lanes = slice(tile * LANES, (tile + 1) * LANES)
+            value = gram[first : first + RUN, lanes]
+            if tile == (first % half) // LANES:
+                sums = gram[size : size + 8, lanes]
+                tail = jnp.where(
+                    first_col,
+                    pltpu.roll(sums, LANES - 7, 1)[0:1],
+                    pltpu.roll(sums, LANES - 5, 1)[1:2],
+                )
+                hidden = value
+                for mask, part in zip(
+                    masks[spot % (LANES // RUN)], (sums[0:1], sums[1:2], tail), strict=True
+                ):
+                    hidden = jnp.where(mask, part, hidden)
+                value = jnp.where(which == first // half, hidden, value)
+            out_ref[place, tile * RUN : (tile + 1) * RUN, :] = value.astype(out_ref.dtype)
+
+
+def send_kernel(rows_ref, flag_ref, plane_ref, send_ref, feat_a, feat_b, land):
+    feats = (feat_a, feat_b)
     per_panel = Y * X // PANELS
     size = per_panel * RUN
     half = size // CORE
     rows, width = rows_ref.shape
     lane = lax.broadcasted_iota(jnp.int32, (8, LANES), 1)
-    for place in range(Y * X):
+    for at, place in enumerate(PLANE_ORDER):
         panel, base = place // per_panel, (place % per_panel) * RUN
-        land[panel, base : base + RUN, :LANES] = plane_ref[place, :RUN]
-        packed = plane_ref[place, RUN:].astype(jnp.float32)
+        land[panel, base : base + RUN, :LANES] = plane_ref[at, :RUN]
+        packed = plane_ref[at, RUN:].astype(jnp.float32)
         pieces = []
         for group in range(ZL):
             rolled = packed if group == 0 else pltpu.roll(packed, LANES - GROUP * group, 1)
@@ -165,13 +169,15 @@
         mask = jnp.where(row == 0, flag, jnp.where(row == 1, 1.0 - flag, 0.0))
         for panel in range(PANELS):
             arg = lax.dot_general(land[panel], wide, NT, preferred_element_type=jnp.float32)
-            feat[panel, :size, at : at + BLOCK] = jnp.exp(arg).astype(jnp.bfloat16)
-            feat[panel, size:, at : at + BLOCK] = mask.astype(jnp.bfloat16)
-    half_gram(1 - lax.axis_index("core"), feat, send_ref, acc)
-
-
-def keep_kernel(feat, keep_ref, acc):
-    half_gram(lax.axis_index("core"), feat, keep_ref, acc)
+            feats[panel][:size, at : at + BLOCK] = jnp.exp(arg).astype(jnp.bfloat16)
+            feats[panel][size:, at : at + BLOCK] = mask.astype(jnp.bfloat16)
+    for panel in range(PANELS):
+        half_gram(1 - lax.axis_index("core"), panel, feats[panel], send_ref)
+
+
+def keep_kernel(feat_a, feat_b, keep_ref):
+    for panel, feat in enumerate((feat_a, feat_b)):
+        half_gram(lax.axis_index("core"), panel, feat, keep_ref)
 
 
 def chip_gram(rows, flag, plane):
@@ -179,18 +185,15 @@
     half = size // CORE
     shape = (Y * X, half // LANES * RUN, LANES)
     count, width = rows.shape
-    acc = pltpu.VMEM((size + MASKS, half), jnp.float32)
+    feat = jax.ShapeDtypeStruct((size + MASKS, count), jnp.bfloat16)
     flops = 2 * count * PANELS * size * half
-    send, feat = call(
+    send, *feats = call(
         send_kernel,
-        (
-            jax.ShapeDtypeStruct(shape, jnp.bfloat16),
-            jax.ShapeDtypeStruct((PANELS, size + MASKS, count), jnp.bfloat16),
-        ),
+        (jax.ShapeDtypeStruct(shape, jnp.bfloat16), feat, feat),
         rows,
         flag,
         plane,
-        scratch=[pltpu.VMEM((PANELS, size, 2 * LANES), jnp.bfloat16), acc],
+        scratch=[pltpu.VMEM((PANELS, size, 2 * LANES), jnp.bfloat16)],
         cost=pl.CostEstimate(
             flops=flops + 4 * count * PANELS * size * width,
             transcendentals=count * PANELS * size,
@@ -202,8 +205,7 @@
     keep = call(
         keep_kernel,
         jax.ShapeDtypeStruct(shape, jnp.float32),
-        feat,
-        scratch=[acc],
+        *feats,
         cost=pl.CostEstimate(flops=flops, transcendentals=0, bytes_accessed=6 << 20),
         vmem=16 << 20,
     )
@@ -220,11 +222,10 @@
         total += terms_ref[place].astype(jnp.float32)
     total = total.astype(jnp.bfloat16)
     tiles = total.shape[0] // RUN
-    for high in range(ZH):
-        for low in range(ZL):
-            for tile in range(tiles):
-                at = tile * RUN + low * OWN
-                out_ref[high * ZL + low, tile * OWN : (tile + 1) * OWN] = total[at : at + OWN]
+    for at, place in enumerate(RING_ORDER):
+        for tile in range(tiles):
+            first = tile * RUN + place % ZL * OWN
+            out_ref[at, tile * OWN : (tile + 1) * OWN] = total[first : first + OWN]
 
 
 def ring_sum_kernel(terms_ref, out_ref):
@@ -276,14 +277,14 @@
         run,
         cost=early,
     )
-    plane = lax.all_to_all(plane, PLANE, 0, 0)
+    plane = lax.all_to_all(plane, PLANE, 0, 0, axis_index_groups=[PLANE_ORDER])
 
     got, keep = chip_gram(covariates, treated.reshape(1, count), plane)
     terms = call(pair_kernel, jax.ShapeDtypeStruct(got.shape, bf16), keep, got)
-    terms = lax.all_to_all(terms, PLANE, 0, 0)
+    terms = lax.all_to_all(terms, PLANE, 0, 0, axis_index_groups=[PLANE_ORDER])
     rows = terms.shape[1] // ZL
     ring = call(plane_sum_kernel, jax.ShapeDtypeStruct((ZH * ZL, rows, LANES), bf16), terms)
-    ring = lax.all_to_all(ring, RING, 0, 0)
+    ring = lax.all_to_all(ring, RING, 0, 0, axis_index_groups=[RING_ORDER])
     ring = call(ring_sum_kernel, jax.ShapeDtypeStruct((rows, LANES), f32), ring)
     both = lax.all_gather(ring, "core", axis=0, tiled=True)
 

time: 82.1 us -> 76.5 us (0.932)
  blocking collectives: 69.2 us -> 63.9 us
    all_to_all x3, blocking collectives: 45.2 us -> 41.1 us  [the longest x1 16 us: on_device(): ring = lax.all_to_all(ring, RING, 0, 0, axis_index_groups=[RING_ORDER])]
    all_gather x1, blocking collectives: 4.75 us -> 3.47 us  [on_device(): both = lax.all_gather(ring, 'core', axis=0, tiled=True)]
where the time goes in v6:
time: 76.5 us; the launch traced here: 76.2 us
  blocking collectives  63.9 us (84%)
  Pallas kernels  5.62 us (7%)
  starting transfers between devices  5.34 us (7%)
    all_to_all x1, blocking collectives, on_device(): run = lax.all_to_all(run, RING, 0, 0, axis_index_groups=run_groups())  19.3 us
    all_to_all x1, blocking collectives, on_device(): ring = lax.all_to_all(ring, RING, 0, 0, axis_index_groups=[RING_ORDER])  16 us
    all_to_all x1, blocking collectives, on_device(): terms = lax.all_to_all(terms, PLANE, 0, 0, axis_index_groups=[PLANE_ORDER])  13.8 us
    all_to_all x1, blocking collectives, on_device(): plane = lax.all_to_all(plane, PLANE, 0, 0, axis_index_groups=[PLANE_ORDER])  11.3 us
    pallas_call x9, Pallas kernels, call(): pl.pallas_call(kernel, in_specs=[pl.BlockSpec(memory_space=space)] * len(...  5.62 us
    ppermute x1, starting transfers between devices, chip_gram(): got = lax.ppermute(send, 'core', [(0, 1), (1, 0)])  5.34 us
    all_gather x1, blocking collectives, on_device(): both = lax.all_gather(ring, 'core', axis=0, tiled=True)  3.47 us
  transfers between devices with their start and end apart: 1, of which 0 were waited for; matrix products, arithmetic and copies ran while one was open for 0% of the time, Pallas kernels for 2%

profile of v6, /device:TPU:1, one launch (start us, length us, event | category | flops | bytes accessed | tf_op | source)
XLA Modules:
  0.0 76.2 jit_solution(17595406172417135383)
XLA Ops:
  0.6 0.0 copy-start
  0.6 0.0 copy-start.1
  0.7 0.6 copy-done
  1.3 0.0 copy-done.1
  1.3 0.1 pack_kernel.1
  1.4 19.3 %all_to_all.20.run_ref = bf16[8,16,128]{2,1,0:T(8,128)(2,1)S(1)} all-to-all(bf16[8,16,128]{2,1,0:T(8,128)(2,1)S(1)} %pack_kernel.1), channel_id=1, replica_groups={{2,6,10,14,16,20,24,28},{0,4,8,12,18,22,26,30},{3,7,11,15,17,21,25,29},..., dimensions={0} | all-to-all | bytes 65536 | tf_op jit(solution)/shard_map/all_to_all | solution.py:273
  20.7 0.0 copy-start.2
  20.7 0.0 copy-start.3
  20.7 11.3 %all_to_all.21.plane_ref = bf16[16,72,128]{2,1,0:T(8,128)(2,1)S(1)} all-to-all(bf16[16,72,128]{2,1,0:T(8,128)(2,1)S(1)} %run_kernel.1), channel_id=1, replica_groups={{320,352,384,416,448,480,0,32,64,96,128,160,192,224,256,288},{321,353,3..., dimensions={0} | all-to-all | bytes 589824 | tf_op jit(solution)/shard_map/all_to_all | solution.py:280
  32.1 0.0 copy-done.2
  32.1 0.0 copy-done.3
  32.1 3.0 %send_kernel.1 = (bf16[16,128,128]{2,1,0:T(8,128)(2,1)S(1)}, bf16[528,2048]{1,0:T(8,128)(2,1)S(1)}, bf16[528,2048]{1,0:T(8,128)(2,1)S(1)}) custom-call(bf16[2048,128]{1,0:T(8,128)(2,1)S(1)} %copy-done.2, s32[1,2048]{1,0:T(1,128)S(1)} %bitcast.5, bf16[16,72,128]{2,1,0:T(8,128)(2,1)S(1)} %all_to_all.21.plane_ref), custom_call_target="tpu_custom_call" | custom-call | flops 2147483648 | bytes 6291456 | tf_op jit(solution)/shard_map/send_kernel/pallas_call | solution.py:36
  35.1 5.3 %collective-permute-start = (bf16[16,128,128]{2,1,0:T(8,128)(2,1)S(1)}, bf16[16,128,128]{2,1,0:T(8,128)(2,1)S(1)}, u32[]{:S(2)}, u32[]{:S(2)}) collective-permute-start(bf16[16,128,128]{2,1,0:T(8,128)(2,1)S(1)} %get-tuple-element.9), channel_id=1, source_target_pairs={{0,1},{1,0},{2,3},{3,2},{4,5},{5,4},{6,7},{7,6},{8,9},{9,8},{10,11... | collective-permute-start | bytes 1572872 | tf_op jit(solution)/shard_map/ppermute | solution.py:204
  40.4 1.5 %keep_kernel.1.keep_ref = f32[16,128,128]{2,1,0:T(8,128)S(1)} custom-call(bf16[528,2048]{1,0:T(8,128)(2,1)S(1)} %get-tuple-element.7.feat_a, bf16[528,2048]{1,0:T(8,128)(2,1)S(1)} %get-tuple-element.8.feat_b), custom_call_target="tpu_custom_call" | custom-call | flops 1073741824 | bytes 6291456 | tf_op jit(solution)/shard_map/keep_kernel/pallas_call | solution.py:36
  41.9 0.0 collective-permute-done.got_ref
  41.9 0.1 pair_kernel.1
  42.0 13.8 %all_to_all.22.terms_ref = bf16[16,128,128]{2,1,0:T(8,128)(2,1)S(1)} all-to-all(bf16[16,128,128]{2,1,0:T(8,128)(2,1)S(1)} %pair_kernel.1), channel_id=1, replica_groups={{320,352,384,416,448,480,0,32,64,96,128,160,192,224,256,288},{321,353,3..., dimensions={0} | all-to-all | bytes 1048576 | tf_op jit(solution)/shard_map/all_to_all | solution.py:284
  55.8 0.1 plane_sum_kernel.1
  55.9 16.0 %all_to_all.23.terms_ref = bf16[16,16,128]{2,1,0:T(8,128)(2,1)S(1)} all-to-all(bf16[16,16,128]{2,1,0:T(8,128)(2,1)S(1)} %plane_sum_kernel.1), channel_id=1, replica_groups={{10,14,18,22,26,30,0,4,8,12,16,20,24,28,2,6},{11,15,19,23,27,31,1,5,9,1..., dimensions={0} | all-to-all | bytes 131072 | tf_op jit(solution)/shard_map/all_to_all | solution.py:287
  71.9 3.5 %all_gather.3.refs_0_ = f32[32,128]{1,0:T(8,128)S(1)} all-gather(f32[16,128]{1,0:T(8,128)S(1)} %ring_sum_kernel.1), channel_id=1, replica_groups=mesh['y'=4,'x'=4,'zl'=8,'zh'=2,'core'=2] {'core'}, dimensions={0}, use_global_device_ids=true | all-gather | bytes 24576 | tf_op jit(solution)/shard_map/all_gather | solution.py:289
  75.4 0.8 %finish.1 = (f32[8,512]{1,0:T(8,128)}, f32[1,8]{1,0:T(1,128)}) custom-call(f32[32,128]{1,0:T(8,128)S(1)} %all_gather.3.refs_0_, bf16[1,8]{1,0:T(2,128)(2,1)S(1)} %bitcast.4), custom_call_target="tpu_custom_call" | custom-call | tf_op jit(solution)/shard_map/finish/pallas_call | solution.py:36
  (3 shorter events, 0.1 us)
Async XLA Ops:
  0.6 0.7 copy-start
  0.6 0.7 copy-start.1
  20.7 11.4 %copy-start.2 = (bf16[2048,128]{1,0:T(8,128)(2,1)S(1)}, bf16[2048,128]{1,0:T(8,128)(2,1)}, u32[]{:S(2)}) copy-start(bf16[2048,128]{1,0:T(8,128)(2,1)} %rows_ref.1) | copy-start | bytes 1572868
  20.7 11.4 %copy-start.3 = (s32[2048]{0:T(1024)S(1)}, s32[2048]{0:T(1024)}, u32[]{:S(2)}) copy-start(s32[2048]{0:T(1024)} %param.5) | copy-start | bytes 24580
  35.1 6.9 %collective-permute-start = (bf16[16,128,128]{2,1,0:T(8,128)(2,1)S(1)}, bf16[16,128,128]{2,1,0:T(8,128)(2,1)S(1)}, u32[]{:S(2)}, u32[]{:S(2)}) collective-permute-start(bf16[16,128,128]{2,1,0:T(8,128)(2,1)S(1)} %get-tuple-element.9), channel_id=1, source_target_pairs={{0,1},{1,0},{2,3},{3,2},{4,5},{5,4},{6,7},{7,6},{8,9},{9,8},{10,11... | collective-permute-start | bytes 1572872 | tf_op jit(solution)/shard_map/ppermute | solution.py:204

commit v7 on v6

--- a/solution.py
+++ b/solution.py
@@ -14,7 +14,7 @@
 MASKS = 16
 BLOCK = 2048
 FIRST = 4
-NEAR_LEAD, RING_LEAD, PLANE_LEAD = 0, 10, 10
+NEAR_LEAD, RING_LEAD, PLANE_LEAD = 0, 9, 10
 NEAR_ORDER = [(NEAR_LEAD + step) % ZL for step in range(ZL)]
 RING_ORDER = [(RING_LEAD + step) % (ZH * ZL) for step in range(ZH * ZL)]
 PLANE_ORDER = [(PLANE_LEAD + step) % (Y * X) for step in range(Y * X)]

time: 76.5 us -> 75.7 us (0.990)
  blocking collectives: 63.9 us -> 63.1 us
    all_to_all x1, blocking collectives: 16 us -> 15.2 us  [on_device(): ring = lax.all_to_all(ring, RING, 0, 0, axis_index_groups=[RING_ORDER])]
where the time goes in v7:
time: 75.7 us; the launch traced here: 75.4 us
  blocking collectives  63.1 us (83%)
  Pallas kernels  5.62 us (7%)
  starting transfers between devices  5.34 us (7%)
    all_to_all x1, blocking collectives, on_device(): run = lax.all_to_all(run, RING, 0, 0, axis_index_groups=run_groups())  19.3 us
    all_to_all x1, blocking collectives, on_device(): ring = lax.all_to_all(ring, RING, 0, 0, axis_index_groups=[RING_ORDER])  15.2 us
    all_to_all x1, blocking collectives, on_device(): terms = lax.all_to_all(terms, PLANE, 0, 0, axis_index_groups=[PLANE_ORDER])  13.8 us
    all_to_all x1, blocking collectives, on_device(): plane = lax.all_to_all(plane, PLANE, 0, 0, axis_index_groups=[PLANE_ORDER])  11.3 us
    pallas_call x9, Pallas kernels, call(): pl.pallas_call(kernel, in_specs=[pl.BlockSpec(memory_space=space)] * len(...  5.62 us
    ppermute x1, starting transfers between devices, chip_gram(): got = lax.ppermute(send, 'core', [(0, 1), (1, 0)])  5.34 us
    all_gather x1, blocking collectives, on_device(): both = lax.all_gather(ring, 'core', axis=0, tiled=True)  3.47 us
  transfers between devices with their start and end apart: 1, of which 0 were waited for; matrix products, arithmetic and copies ran while one was open for 0% of the time, Pallas kernels for 2%

profile of v7, /device:TPU:1, one launch (start us, length us, event | category | flops | bytes accessed | tf_op | source)
XLA Modules:
  0.0 75.4 jit_solution(15738513445049541130)
XLA Ops:
  0.6 0.0 copy-start
  0.6 0.0 copy-start.1
  0.7 0.6 copy-done
  1.3 0.0 copy-done.1
  1.3 0.1 pack_kernel.1
  1.4 19.3 %all_to_all.20.run_ref = bf16[8,16,128]{2,1,0:T(8,128)(2,1)S(1)} all-to-all(bf16[8,16,128]{2,1,0:T(8,128)(2,1)S(1)} %pack_kernel.1), channel_id=1, replica_groups={{2,6,10,14,16,20,24,28},{0,4,8,12,18,22,26,30},{3,7,11,15,17,21,25,29},..., dimensions={0} | all-to-all | bytes 65536 | tf_op jit(solution)/shard_map/all_to_all | solution.py:273
  20.7 0.0 copy-start.2
  20.7 0.0 copy-start.3
  20.7 11.3 %all_to_all.21.plane_ref = bf16[16,72,128]{2,1,0:T(8,128)(2,1)S(1)} all-to-all(bf16[16,72,128]{2,1,0:T(8,128)(2,1)S(1)} %run_kernel.1), channel_id=1, replica_groups={{320,352,384,416,448,480,0,32,64,96,128,160,192,224,256,288},{321,353,3..., dimensions={0} | all-to-all | bytes 589824 | tf_op jit(solution)/shard_map/all_to_all | solution.py:280
  32.1 0.0 copy-done.2
  32.1 0.0 copy-done.3
  32.1 3.0 %send_kernel.1 = (bf16[16,128,128]{2,1,0:T(8,128)(2,1)S(1)}, bf16[528,2048]{1,0:T(8,128)(2,1)S(1)}, bf16[528,2048]{1,0:T(8,128)(2,1)S(1)}) custom-call(bf16[2048,128]{1,0:T(8,128)(2,1)S(1)} %copy-done.2, s32[1,2048]{1,0:T(1,128)S(1)} %bitcast.5, bf16[16,72,128]{2,1,0:T(8,128)(2,1)S(1)} %all_to_all.21.plane_ref), custom_call_target="tpu_custom_call" | custom-call | flops 2147483648 | bytes 6291456 | tf_op jit(solution)/shard_map/send_kernel/pallas_call | solution.py:36
  35.1 5.3 %collective-permute-start = (bf16[16,128,128]{2,1,0:T(8,128)(2,1)S(1)}, bf16[16,128,128]{2,1,0:T(8,128)(2,1)S(1)}, u32[]{:S(2)}, u32[]{:S(2)}) collective-permute-start(bf16[16,128,128]{2,1,0:T(8,128)(2,1)S(1)} %get-tuple-element.9), channel_id=1, source_target_pairs={{0,1},{1,0},{2,3},{3,2},{4,5},{5,4},{6,7},{7,6},{8,9},{9,8},{10,11... | collective-permute-start | bytes 1572872 | tf_op jit(solution)/shard_map/ppermute | solution.py:204
  40.4 1.5 %keep_kernel.1.keep_ref = f32[16,128,128]{2,1,0:T(8,128)S(1)} custom-call(bf16[528,2048]{1,0:T(8,128)(2,1)S(1)} %get-tuple-element.7.feat_a, bf16[528,2048]{1,0:T(8,128)(2,1)S(1)} %get-tuple-element.8.feat_b), custom_call_target="tpu_custom_call" | custom-call | flops 1073741824 | bytes 6291456 | tf_op jit(solution)/shard_map/keep_kernel/pallas_call | solution.py:36
  41.9 0.0 collective-permute-done.got_ref
  41.9 0.1 pair_kernel.1
  42.0 13.8 %all_to_all.22.terms_ref = bf16[16,128,128]{2,1,0:T(8,128)(2,1)S(1)} all-to-all(bf16[16,128,128]{2,1,0:T(8,128)(2,1)S(1)} %pair_kernel.1), channel_id=1, replica_groups={{320,352,384,416,448,480,0,32,64,96,128,160,192,224,256,288},{321,353,3..., dimensions={0} | all-to-all | bytes 1048576 | tf_op jit(solution)/shard_map/all_to_all | solution.py:284
  55.8 0.1 plane_sum_kernel.1
  55.9 15.2 %all_to_all.23.terms_ref = bf16[16,16,128]{2,1,0:T(8,128)(2,1)S(1)} all-to-all(bf16[16,16,128]{2,1,0:T(8,128)(2,1)S(1)} %plane_sum_kernel.1), channel_id=1, replica_groups={{6,10,14,18,22,26,30,0,4,8,12,16,20,24,28,2},{7,11,15,19,23,27,31,1,5,9..., dimensions={0} | all-to-all | bytes 131072 | tf_op jit(solution)/shard_map/all_to_all | solution.py:287
  71.1 3.5 %all_gather.3.refs_0_ = f32[32,128]{1,0:T(8,128)S(1)} all-gather(f32[16,128]{1,0:T(8,128)S(1)} %ring_sum_kernel.1), channel_id=1, replica_groups=mesh['y'=4,'x'=4,'zl'=8,'zh'=2,'core'=2] {'core'}, dimensions={0}, use_global_device_ids=true | all-gather | bytes 24576 | tf_op jit(solution)/shard_map/all_gather | solution.py:289
  74.6 0.8 %finish.1 = (f32[8,512]{1,0:T(8,128)}, f32[1,8]{1,0:T(1,128)}) custom-call(f32[32,128]{1,0:T(8,128)S(1)} %all_gather.3.refs_0_, bf16[1,8]{1,0:T(2,128)(2,1)S(1)} %bitcast.4), custom_call_target="tpu_custom_call" | custom-call | tf_op jit(solution)/shard_map/finish/pallas_call | solution.py:36
  (3 shorter events, 0.1 us)
Async XLA Ops:
  0.6 0.7 copy-start
  0.6 0.7 copy-start.1
  20.7 11.4 %copy-start.2 = (bf16[2048,128]{1,0:T(8,128)(2,1)S(1)}, bf16[2048,128]{1,0:T(8,128)(2,1)}, u32[]{:S(2)}) copy-start(bf16[2048,128]{1,0:T(8,128)(2,1)} %rows_ref.1) | copy-start | bytes 1572868
  20.7 11.4 %copy-start.3 = (s32[2048]{0:T(1024)S(1)}, s32[2048]{0:T(1024)}, u32[]{:S(2)}) copy-start(s32[2048]{0:T(1024)} %param.5) | copy-start | bytes 24580
  35.1 6.9 %collective-permute-start = (bf16[16,128,128]{2,1,0:T(8,128)(2,1)S(1)}, bf16[16,128,128]{2,1,0:T(8,128)(2,1)S(1)}, u32[]{:S(2)}, u32[]{:S(2)}) collective-permute-start(bf16[16,128,128]{2,1,0:T(8,128)(2,1)S(1)} %get-tuple-element.9), channel_id=1, source_target_pairs={{0,1},{1,0},{2,3},{3,2},{4,5},{5,4},{6,7},{7,6},{8,9},{9,8},{10,11... | collective-permute-start | bytes 1572872 | tf_op jit(solution)/shard_map/ppermute | solution.py:204

commit v8 on v7

--- a/solution.py
+++ b/solution.py
@@ -13,7 +13,7 @@
 RUN = ZL * OWN
 MASKS = 16
 BLOCK = 2048
-FIRST = 4
+FIRST = 5
 NEAR_LEAD, RING_LEAD, PLANE_LEAD = 0, 9, 10
 NEAR_ORDER = [(NEAR_LEAD + step) % ZL for step in range(ZL)]
 RING_ORDER = [(RING_LEAD + step) % (ZH * ZL) for step in range(ZH * ZL)]

time: 75.7 us -> 74.9 us (0.989)
  blocking collectives: 63.1 us -> 62.2 us
where the time goes in v8:
time: 74.9 us; the launch traced here: 74.6 us
  blocking collectives  62.2 us (83%)
  Pallas kernels  5.63 us (8%)
  starting transfers between devices  5.34 us (7%)
    all_to_all x1, blocking collectives, on_device(): run = lax.all_to_all(run, RING, 0, 0, axis_index_groups=run_groups())  18.8 us
    all_to_all x1, blocking collectives, on_device(): ring = lax.all_to_all(ring, RING, 0, 0, axis_index_groups=[RING_ORDER])  14.8 us
    all_to_all x1, blocking collectives, on_device(): terms = lax.all_to_all(terms, PLANE, 0, 0, axis_index_groups=[PLANE_ORDER])  13.8 us
    all_to_all x1, blocking collectives, on_device(): plane = lax.all_to_all(plane, PLANE, 0, 0, axis_index_groups=[PLANE_ORDER])  11.3 us
    pallas_call x9, Pallas kernels, call(): pl.pallas_call(kernel, in_specs=[pl.BlockSpec(memory_space=space)] * len(...  5.63 us
    ppermute x1, starting transfers between devices, chip_gram(): got = lax.ppermute(send, 'core', [(0, 1), (1, 0)])  5.34 us
    all_gather x1, blocking collectives, on_device(): both = lax.all_gather(ring, 'core', axis=0, tiled=True)  3.47 us
  transfers between devices with their start and end apart: 1, of which 0 were waited for; matrix products, arithmetic and copies ran while one was open for 0% of the time, Pallas kernels for 2%

profile of v8, /device:TPU:1, one launch (start us, length us, event | category | flops | bytes accessed | tf_op | source)
XLA Modules:
  0.0 74.6 jit_solution(10809172255017228544)
XLA Ops:
  0.6 0.0 copy-start
  0.6 0.0 copy-start.1
  0.7 0.6 copy-done
  1.3 0.0 copy-done.1
  1.3 0.1 pack_kernel.1
  1.4 18.8 %all_to_all.20.run_ref = bf16[8,16,128]{2,1,0:T(8,128)(2,1)S(1)} all-to-all(bf16[8,16,128]{2,1,0:T(8,128)(2,1)S(1)} %pack_kernel.1), channel_id=1, replica_groups={{2,6,10,14,18,20,24,28},{0,4,8,12,16,22,26,30},{3,7,11,15,19,21,25,29},..., dimensions={0} | all-to-all | bytes 65536 | tf_op jit(solution)/shard_map/all_to_all | solution.py:273
  20.3 0.0 copy-start.2
  20.3 0.0 copy-start.3
  20.3 11.3 %all_to_all.21.plane_ref = bf16[16,72,128]{2,1,0:T(8,128)(2,1)S(1)} all-to-all(bf16[16,72,128]{2,1,0:T(8,128)(2,1)S(1)} %run_kernel.1), channel_id=1, replica_groups={{320,352,384,416,448,480,0,32,64,96,128,160,192,224,256,288},{321,353,3..., dimensions={0} | all-to-all | bytes 589824 | tf_op jit(solution)/shard_map/all_to_all | solution.py:280
  31.6 0.0 copy-done.2
  31.6 0.0 copy-done.3
  31.6 3.0 %send_kernel.1 = (bf16[16,128,128]{2,1,0:T(8,128)(2,1)S(1)}, bf16[528,2048]{1,0:T(8,128)(2,1)S(1)}, bf16[528,2048]{1,0:T(8,128)(2,1)S(1)}) custom-call(bf16[2048,128]{1,0:T(8,128)(2,1)S(1)} %copy-done.2, s32[1,2048]{1,0:T(1,128)S(1)} %bitcast.5, bf16[16,72,128]{2,1,0:T(8,128)(2,1)S(1)} %all_to_all.21.plane_ref), custom_call_target="tpu_custom_call" | custom-call | flops 2147483648 | bytes 6291456 | tf_op jit(solution)/shard_map/send_kernel/pallas_call | solution.py:36
  34.6 5.3 %collective-permute-start = (bf16[16,128,128]{2,1,0:T(8,128)(2,1)S(1)}, bf16[16,128,128]{2,1,0:T(8,128)(2,1)S(1)}, u32[]{:S(2)}, u32[]{:S(2)}) collective-permute-start(bf16[16,128,128]{2,1,0:T(8,128)(2,1)S(1)} %get-tuple-element.9), channel_id=1, source_target_pairs={{0,1},{1,0},{2,3},{3,2},{4,5},{5,4},{6,7},{7,6},{8,9},{9,8},{10,11... | collective-permute-start | bytes 1572872 | tf_op jit(solution)/shard_map/ppermute | solution.py:204
  40.0 1.5 %keep_kernel.1.keep_ref = f32[16,128,128]{2,1,0:T(8,128)S(1)} custom-call(bf16[528,2048]{1,0:T(8,128)(2,1)S(1)} %get-tuple-element.7.feat_a, bf16[528,2048]{1,0:T(8,128)(2,1)S(1)} %get-tuple-element.8.feat_b), custom_call_target="tpu_custom_call" | custom-call | flops 1073741824 | bytes 6291456 | tf_op jit(solution)/shard_map/keep_kernel/pallas_call | solution.py:36
  41.5 0.0 collective-permute-done.got_ref
  41.5 0.1 pair_kernel.1
  41.6 13.8 %all_to_all.22.terms_ref = bf16[16,128,128]{2,1,0:T(8,128)(2,1)S(1)} all-to-all(bf16[16,128,128]{2,1,0:T(8,128)(2,1)S(1)} %pair_kernel.1), channel_id=1, replica_groups={{320,352,384,416,448,480,0,32,64,96,128,160,192,224,256,288},{321,353,3..., dimensions={0} | all-to-all | bytes 1048576 | tf_op jit(solution)/shard_map/all_to_all | solution.py:284
  55.4 0.1 plane_sum_kernel.1
  55.5 14.8 %all_to_all.23.terms_ref = bf16[16,16,128]{2,1,0:T(8,128)(2,1)S(1)} all-to-all(bf16[16,16,128]{2,1,0:T(8,128)(2,1)S(1)} %plane_sum_kernel.1), channel_id=1, replica_groups={{6,10,14,18,22,26,30,0,4,8,12,16,20,24,28,2},{7,11,15,19,23,27,31,1,5,9..., dimensions={0} | all-to-all | bytes 131072 | tf_op jit(solution)/shard_map/all_to_all | solution.py:287
  70.3 3.5 %all_gather.3.refs_0_ = f32[32,128]{1,0:T(8,128)S(1)} all-gather(f32[16,128]{1,0:T(8,128)S(1)} %ring_sum_kernel.1), channel_id=1, replica_groups=mesh['y'=4,'x'=4,'zl'=8,'zh'=2,'core'=2] {'core'}, dimensions={0}, use_global_device_ids=true | all-gather | bytes 24576 | tf_op jit(solution)/shard_map/all_gather | solution.py:289
  73.8 0.8 %finish.1 = (f32[8,512]{1,0:T(8,128)}, f32[1,8]{1,0:T(1,128)}) custom-call(f32[32,128]{1,0:T(8,128)S(1)} %all_gather.3.refs_0_, bf16[1,8]{1,0:T(2,128)(2,1)S(1)} %bitcast.4), custom_call_target="tpu_custom_call" | custom-call | tf_op jit(solution)/shard_map/finish/pallas_call | solution.py:36
  (3 shorter events, 0.1 us)
Async XLA Ops:
  0.6 0.7 copy-start
  0.6 0.7 copy-start.1
  20.3 11.4 %copy-start.2 = (bf16[2048,128]{1,0:T(8,128)(2,1)S(1)}, bf16[2048,128]{1,0:T(8,128)(2,1)}, u32[]{:S(2)}) copy-start(bf16[2048,128]{1,0:T(8,128)(2,1)} %rows_ref.1) | copy-start | bytes 1572868
  20.3 11.4 %copy-start.3 = (s32[2048]{0:T(1024)S(1)}, s32[2048]{0:T(1024)}, u32[]{:S(2)}) copy-start(s32[2048]{0:T(1024)} %param.5) | copy-start | bytes 24580
  34.6 6.9 %collective-permute-start = (bf16[16,128,128]{2,1,0:T(8,128)(2,1)S(1)}, bf16[16,128,128]{2,1,0:T(8,128)(2,1)S(1)}, u32[]{:S(2)}, u32[]{:S(2)}) collective-permute-start(bf16[16,128,128]{2,1,0:T(8,128)(2,1)S(1)} %get-tuple-element.9), channel_id=1, source_target_pairs={{0,1},{1,0},{2,3},{3,2},{4,5},{5,4},{6,7},{7,6},{8,9},{9,8},{10,11... | collective-permute-start | bytes 1572872 | tf_op jit(solution)/shard_map/ppermute | solution.py:204
